TPU v7x, 256 devices: a whole 4x4x8 slice. The times are simulated.
256 devices in a mesh: section: 2 (over core), expert: 64 (over y, x, z_lo), head: 2 (over z_hi).
Axes of the slice: x: 4, y: 4, z: 8 (z_hi: 2, z_lo: 4; z = z_hi * 4 + z_lo), core: 2. Of those that a mesh axis runs over, the one named last changes fastest.
Arguments:
- boundary: bfloat16 [2, 2, 8192, 768], P('section', None, 'expert', 'head'), may hold values from -6 to 6
- norm_gain: float32 [2, 768], P('section'), may hold values from 0.25 to 1.75
- gate_prob: float32 [2, 2, 8192], P('section', None, 'expert'), may hold values from 0.25 to 1
- expert_ids: int32 [2, 2, 8192], P('section', None, 'expert'), may hold values from 0 to 63, as said below
- slot_ids: int32 [2, 2, 8192], P('section', None, 'expert'), may hold values from 0 to 4, as said below
- weight_in: bfloat16 [2, 64, 768, 3072], P('section', 'expert', None, 'head'), may hold values from -0.21875 to 0.21875
- weight_out: bfloat16 [2, 64, 3072, 768], P('section', 'expert', 'head'), may hold values from -0.109375 to 0.109375
Outputs:
- boundary_out: bfloat16 [2, 2, 8192, 768], P('section', None, 'expert', 'head')
- grad_in: bfloat16 [2, 64, 768, 3072], P('section', 'expert', None, 'head')
- grad_out: bfloat16 [2, 64, 3072, 768], P('section', 'expert', 'head')
Inputs may be any that keep to these rules, and one draw needn't show every extreme that they name: `expert_ids`: within each layer and micro-batch, tokens are taken in blocks of 128 (the tokens of one index of expert); in every block one expert, the same for all blocks of that layer and micro-batch, is named by more than 4 tokens. `slot_ids`: A token's slot is the number of earlier tokens of its block that name the same expert, capped at 4; 4 means the token is dropped. So at most 4 tokens of a block hold a slot below 4 at one expert, and in every layer and micro-batch one expert has all 4 slots filled from every block.
All inputs are finite; a program needn't handle non-finite values.
Results may differ from a plain program's by a relative error of at most 0.008.
Values may be sent and summed in bfloat16 or wider, within the bound.
No kernel may reach another device: no remote copies, remote signals or barrier semaphores. Data moves between devices by JAX's collectives and lax.ppermute only.
A program may use at most 128 MiB of HBM per device.

v0:
```python
import functools

import jax
import jax.numpy as jnp
from jax import lax
from jax.experimental import pallas as pl
from jax.experimental.pallas import tpu as pltpu
from jax.sharding import PartitionSpec as P

EPSILON = 1e-06
ROOT_COEF = 0.7978845608
CUBE_COEF = 0.044715
VMEM_LIMIT = 40 * 1024 * 1024
BF16, F32 = jnp.bfloat16, jnp.float32


def activate(v):
    sq = v * v
    th = jnp.tanh(ROOT_COEF * (v + CUBE_COEF * sq * v))
    up = 0.5 * (1.0 + th)
    return th, sq, up


def act_of(v):
    _, _, up = activate(v)
    return v * up


def act_and_slope(v):
    th, sq, up = activate(v)
    slope = up + 0.5 * v * (1.0 - th * th) * (ROOT_COEF + (3.0 * CUBE_COEF * ROOT_COEF) * sq)
    return v * up, slope


def dot(a, b, dims=((1,), (0,))):
    return lax.dot_general(a, b, (dims, ((), ())), preferred_element_type=F32)


def call(body, outs, ins, flops, grid=(), in_specs=None, out_specs=None, scratch=(), name=None):
    moved = sum(a.size * a.dtype.itemsize for a in ins)
    moved += sum(s.size * s.dtype.itemsize for s in outs)
    kwargs = {}
    if grid:
        kwargs = dict(grid=grid, in_specs=in_specs, out_specs=out_specs)
    return pl.pallas_call(
        body,
        out_shape=outs,
        scratch_shapes=scratch,
        compiler_params=pltpu.CompilerParams(vmem_limit_bytes=VMEM_LIMIT),
        cost_estimate=pl.CostEstimate(flops=flops, bytes_accessed=moved, transcendentals=0),
        name=name,
        **kwargs,
    )(*ins)


def struct(shape, dtype):
    return jax.ShapeDtypeStruct(shape, dtype)


def one_hot(ids, slots, experts, cap):
    micro, tokens = ids.shape
    per = micro * cap
    target = jnp.where(slots < cap, ids * per + slots, -1 - cap * micro)
    pieces = [target[m : m + 1] + m * cap for m in range(micro)]
    target = jnp.concatenate(pieces, axis=1)
    rows = lax.broadcasted_iota(jnp.int32, (experts * per, micro * tokens), 0)
    return (rows == target).astype(F32).astype(BF16)


def column(rows):
    flat = jnp.concatenate([rows[m : m + 1] for m in range(rows.shape[0])], axis=1)
    return jnp.transpose(jnp.broadcast_to(flat, (8, flat.shape[1])))[:, :1]


def place_body(scaled, cap, *refs):
    if scaled:
        tok, ids, slots, prob, out = refs
    else:
        tok, ids, slots, out = refs
    experts, heads, per, half = out.shape
    tokens = tok[...].reshape(-1, half)
    if scaled:
        tokens = (column(prob[...]) * tokens.astype(F32)).astype(BF16)
    hot = one_hot(ids[...], slots[...], experts, cap)
    rows = dot(hot, tokens).reshape(experts, per, half).astype(BF16)
    for h in range(heads):
        out[:, h] = rows


def place(tokens, ids, slots, prob, experts, cap):
    micro, count, half = tokens.shape
    out = struct((experts, 2, micro * cap, half), BF16)
    ins = (tokens, ids, slots) + (() if prob is None else (prob,))
    flops = 2 * experts * micro * cap * micro * count * half
    return call(functools.partial(place_body, prob is not None, cap), [out], ins, flops, name="place")[0]


def gather_body(forward, cap, *refs):
    if forward:
        got, ids, slots, prob, base, out = refs
    else:
        got, ids, slots, base, out = refs
    experts, heads, per, half = got.shape
    hot = one_hot(ids[...], slots[...], experts, cap)
    first = got[:, 0].astype(F32).reshape(experts * per, half)
    second = got[:, 1].astype(F32).reshape(experts * per, half)
    if forward:
        picked = dot(hot, (first + second).astype(BF16), ((0,), (0,)))
        picked = column(prob[...]) * picked
    else:
        picked = dot(hot, first.astype(BF16), ((0,), (0,))) + dot(hot, second.astype(BF16), ((0,), (0,)))
    total = base[...].reshape(-1, half).astype(F32) + picked
    out[...] = total.astype(BF16).reshape(out.shape)


def gather(got, ids, slots, prob, base, cap):
    ins = (got, ids, slots) + (() if prob is None else (prob,)) + (base,)
    flops = 2 * got.shape[0] * got.shape[2] * base.size
    return call(
        functools.partial(gather_body, prob is not None, cap), [struct(base.shape, BF16)], ins, flops, name="gather"
    )[0]


def rows_of(ref):
    experts, heads, per, half = ref.shape
    return [ref[:, h].astype(F32).reshape(experts * per, half) for h in range(heads)]


def inverse(parts, width):
    total = sum(jnp.sum(v * v, axis=1, keepdims=True) for v in parts)
    return lax.rsqrt(total * (1.0 / width) + EPSILON)


def fill_normed(rows_ref, gain_ref, normed_ref):
    parts = rows_of(rows_ref)
    half = parts[0].shape[1]
    scale = inverse(parts, 2 * half)
    for h, v in enumerate(parts):
        cols = pl.ds(h * half, half)
        normed_ref[:, cols] = (v * scale * gain_ref[:, cols]).astype(BF16)


def spread(total_ref, out_ref):
    experts, heads, per, half = out_ref.shape
    for h in range(heads):
        piece = total_ref[:, pl.ds(h * half, half)]
        out_ref[:, h] = piece.reshape(experts, per, half).astype(BF16)


def spread_norm_grad(total_ref, rows_ref, gain_ref, out_ref):
    experts, heads, per, half = out_ref.shape
    parts = rows_of(rows_ref)
    scale = inverse(parts, heads * half)
    grads = [total_ref[:, pl.ds(h * half, half)] * gain_ref[:, pl.ds(h * half, half)] for h in range(heads)]
    cross = sum(jnp.sum(g * v, axis=1, keepdims=True) for g, v in zip(grads, parts))
    factor = scale * scale * scale * cross * (1.0 / (heads * half))
    for h in range(heads):
        piece = scale * grads[h] - parts[h] * factor
        out_ref[:, h] = piece.reshape(experts, per, half).astype(BF16)


def forward_body(rows, gain, w_in, w_out, out, pre_out, act_out, normed, total):
    step = pl.program_id(0)

    @pl.when(step == 0)
    def _():
        fill_normed(rows, gain, normed)

    pre = dot(normed[...], w_in[...])
    pre_out[...] = pre
    act = act_of(pre).astype(BF16)
    act_out[...] = act
    part = dot(act, w_out[...])

    @pl.when(step == 0)
    def _():
        total[...] = part

    @pl.when(step > 0)
    def _():
        total[...] += part

    @pl.when(step == pl.num_programs(0) - 1)
    def _():
        spread(total, out)


def whole(shape):
    return pl.BlockSpec(shape, lambda j: (0,) * len(shape))


CHUNK = 512


def sizes(rows, w_in):
    count = rows.shape[0] * rows.shape[2]
    width, hidden = w_in.shape
    return count, width, hidden


def expert_forward(rows, gain, w_in, w_out):
    count, width, hidden = sizes(rows, w_in)
    chunk = CHUNK
    cols = pl.BlockSpec((count, chunk), lambda j: (0, j))
    return call(
        forward_body,
        [
            struct(rows.shape, BF16),
            struct((count, hidden), F32),
            struct((count, hidden), BF16),
            struct((count, width), BF16),
        ],
        (rows, gain, w_in, w_out),
        4 * count * width * hidden,
        grid=(hidden // chunk,),
        in_specs=[
            whole(rows.shape),
            whole(gain.shape),
            pl.BlockSpec((width, chunk), lambda j: (0, j)),
            pl.BlockSpec((chunk, width), lambda j: (j, 0)),
        ],
        out_specs=[whole(rows.shape), cols, cols, whole((count, width))],
        scratch=[pltpu.VMEM((count, width), F32)],
        name="expert_forward",
    )


def grad_act_body(grads, w_out, out, flat):
    @pl.when(pl.program_id(0) == 0)
    def _():
        half = grads.shape[3]
        for h, v in enumerate(rows_of(grads)):
            flat[:, pl.ds(h * half, half)] = v.astype(BF16)

    out[...] = dot(flat[...], w_out[...], ((1,), (1,)))


def grad_act_early(grads, w_out):
    hidden, width = w_out.shape
    count = grads.shape[0] * grads.shape[2]
    chunk = CHUNK
    return call(
        grad_act_body,
        [struct((count, hidden), F32), struct((count, width), BF16)],
        (grads, w_out),
        2 * count * width * hidden,
        grid=(hidden // chunk,),
        in_specs=[whole(grads.shape), pl.BlockSpec((chunk, width), lambda j: (j, 0))],
        out_specs=[pl.BlockSpec((count, chunk), lambda j: (0, j)), whole((count, width))],
        name="grad_act",
    )


def both_body(rows, gain, w_in, grad_act, out, act_out, pre_grad_out, normed, total):
    step = pl.program_id(0)

    @pl.when(step == 0)
    def _():
        fill_normed(rows, gain, normed)

    weight = w_in[...]
    act, slope = act_and_slope(dot(normed[...], weight))
    act_out[...] = act.astype(BF16)
    pre_grad = (grad_act[...] * slope).astype(BF16)
    pre_grad_out[...] = pre_grad
    part = dot(pre_grad, weight, ((1,), (1,)))

    @pl.when(step == 0)
    def _():
        total[...] = part

    @pl.when(step > 0)
    def _():
        total[...] += part

    @pl.when(step == pl.num_programs(0) - 1)
    def _():
        spread_norm_grad(total, rows, gain, out)


def expert_both(rows, gain, w_in, grad_act):
    count, width, hidden = sizes(rows, w_in)
    chunk = CHUNK
    cols = pl.BlockSpec((count, chunk), lambda j: (0, j))
    return call(
        both_body,
        [
            struct(rows.shape, BF16),
            struct((count, hidden), BF16),
            struct((count, hidden), BF16),
            struct((count, width), BF16),
        ],
        (rows, gain, w_in, grad_act),
        4 * count * width * hidden,
        grid=(hidden // chunk,),
        in_specs=[
            whole(rows.shape),
            whole(gain.shape),
            pl.BlockSpec((width, chunk), lambda j: (0, j)),
            cols,
        ],
        out_specs=[whole(rows.shape), cols, cols, whole((count, width))],
        scratch=[pltpu.VMEM((count, width), F32)],
        name="expert_both",
    )


def out_body(act, w_out, out, total):
    step = pl.program_id(0)
    part = dot(act[...], w_out[...])

    @pl.when(step == 0)
    def _():
        total[...] = part

    @pl.when(step > 0)
    def _():
        total[...] += part

    @pl.when(step == pl.num_programs(0) - 1)
    def _():
        spread(total, out)


def expert_out(act, w_out, shape):
    count, hidden = act.shape
    width = w_out.shape[1]
    chunk = CHUNK
    return call(
        out_body,
        [struct(shape, BF16)],
        (act, w_out),
        2 * count * width * hidden,
        grid=(hidden // chunk,),
        in_specs=[
            pl.BlockSpec((count, chunk), lambda j: (0, j)),
            pl.BlockSpec((chunk, width), lambda j: (j, 0)),
        ],
        out_specs=[whole(shape)],
        scratch=[pltpu.VMEM((count, width), F32)],
        name="expert_out",
    )[0]


def backward_body(grads, slope, w_in, w_out, rows, gain, out, pre_grad_out, flat, total):
    step = pl.program_id(0)

    @pl.when(step == 0)
    def _():
        half = grads.shape[3]
        for h, v in enumerate(rows_of(grads)):
            flat[:, pl.ds(h * half, half)] = v.astype(BF16)

    grad_act = dot(flat[...], w_out[...], ((1,), (1,)))
    pre_grad = (grad_act * slope[...]).astype(BF16)
    pre_grad_out[...] = pre_grad
    part = dot(pre_grad, w_in[...], ((1,), (1,)))

    @pl.when(step == 0)
    def _():
        total[...] = part

    @pl.when(step > 0)
    def _():
        total[...] += part

    @pl.when(step == pl.num_programs(0) - 1)
    def _():
        spread_norm_grad(total, rows, gain, out)


def expert_backward(grads, slope, w_in, w_out, rows, gain):
    count, width, hidden = sizes(rows, w_in)
    chunk = CHUNK
    cols = pl.BlockSpec((count, chunk), lambda j: (0, j))
    return call(
        backward_body,
        [struct(rows.shape, BF16), struct((count, hidden), BF16), struct((count, width), BF16)],
        (grads, slope, w_in, w_out, rows, gain),
        4 * count * width * hidden,
        grid=(hidden // chunk,),
        in_specs=[
            whole(grads.shape),
            cols,
            pl.BlockSpec((width, chunk), lambda j: (0, j)),
            pl.BlockSpec((chunk, width), lambda j: (j, 0)),
            whole(rows.shape),
            whole(gain.shape),
        ],
        out_specs=[whole(rows.shape), cols, whole((count, width))],
        scratch=[pltpu.VMEM((count, width), F32)],
        name="expert_backward",
    )


def weight_grad_body(normed, pre_grad, act, flat, first, second):
    first[...] = dot(normed[...], pre_grad[...], ((0,), (0,))).astype(BF16)
    second[...] = dot(act[...], flat[...], ((0,), (0,))).astype(BF16)


def weight_grads(normed, pre_grad, act, flat):
    count, width = normed.shape
    hidden = act.shape[1]
    chunk = CHUNK
    cols = pl.BlockSpec((count, chunk), lambda j: (0, j))
    return call(
        weight_grad_body,
        [struct((width, hidden), BF16), struct((hidden, width), BF16)],
        (normed, pre_grad, act, flat),
        4 * count * width * hidden,
        grid=(hidden // chunk,),
        in_specs=[whole(normed.shape), cols, cols, whole(flat.shape)],
        out_specs=[
            pl.BlockSpec((width, chunk), lambda j: (0, j)),
            pl.BlockSpec((chunk, width), lambda j: (j, 0)),
        ],
        name="weight_grads",
    )


def exchange(blocks):
    experts, heads, per, half = blocks.shape
    flat = blocks.reshape(experts * heads, per, half)
    return lax.all_to_all(flat, ("expert", "head"), 0, 0, tiled=True).reshape(blocks.shape)


def swap(block):
    count = lax.axis_size("section")
    return lax.ppermute(block, "section", [(i, (i + 1) % count) for i in range(count)])


def on_device(boundary, norm_gain, gate_prob, expert_ids, slot_ids, weight_in, weight_out):
    experts = lax.axis_size("expert")
    local = boundary[0]
    micro, count, half = local.shape
    cap = 2 * count // experts
    w_in = weight_in[0, 0]
    w_out = weight_out[0, 0]
    width, hidden = w_in.shape
    ids, slots, prob = expert_ids[0], slot_ids[0], gate_prob[0]
    rows_shape = (experts, 2, micro * cap, half)
    rows_count = experts * micro * cap
    first = lax.axis_index("section") == 0

    def stage_one_lower():
        rows = exchange(place(local, ids, slots, None, experts, cap))
        part, pre, act, normed = expert_forward(rows, norm_gain, w_in, w_out)
        hid = gather(exchange(part), ids, slots, prob, local, cap)
        return hid, rows, pre, act, normed

    def stage_one_upper():
        grads = exchange(place(local, ids, slots, prob, experts, cap))
        grad_act, flat = grad_act_early(grads, w_out)
        return local, grads, grad_act, jnp.zeros((rows_count, hidden), BF16), flat

    sent, rows_one, wide, act_one, flat_one = lax.cond(first, stage_one_lower, stage_one_upper)
    hid = swap(sent)

    def stage_two_lower():
        slope = act_and_slope(wide)[1]
        return local, slope, rows_one, act_one, jnp.zeros((rows_count, hidden), BF16), flat_one

    def stage_two_upper():
        rows = exchange(place(hid, ids, slots, None, experts, cap))
        back, act, pre_grad, normed = expert_both(rows, norm_gain, w_in, wide)
        got = exchange(back)
        part = expert_out(act, w_out, rows_shape)
        grad_hid = gather(got, ids, slots, None, local, cap)
        return grad_hid, wide, part, act, pre_grad, normed

    sent, slope, part, act, pre_grad, normed = lax.cond(first, stage_two_lower, stage_two_upper)
    grad_hid = swap(sent)

    def stage_three_lower():
        grads = exchange(place(grad_hid, ids, slots, prob, experts, cap))
        back, pre_grad_low, flat = expert_backward(grads, slope, w_in, w_out, part, norm_gain)
        got = exchange(back)
        first_grad, second_grad = weight_grads(normed, pre_grad_low, act, flat)
        result = gather(got, ids, slots, None, grad_hid, cap)
        return result, first_grad, second_grad

    def stage_three_upper():
        got = exchange(part)
        first_grad, second_grad = weight_grads(normed, pre_grad, act, flat_one)
        result = gather(got, ids, slots, prob, hid, cap)
        return result, first_grad, second_grad

    result, first_grad, second_grad = lax.cond(first, stage_three_lower, stage_three_upper)
    return result[None], first_grad[None, None], second_grad[None, None]


def solution(mesh):
    placed = (
        P("section", None, "expert", "head"),
        P("section", None),
        P("section", None, "expert"),
        P("section", None, "expert"),
        P("section", None, "expert"),
        P("section", "expert", None, "head"),
        P("section", "expert", "head", None),
    )
    return jax.shard_map(
        on_device,
        mesh=mesh,
        in_specs=placed,
        out_specs=(
            P("section", None, "expert", "head"),
            P("section", "expert", None, "head"),
            P("section", "expert", "head", None),
        ),
        check_vma=False,
    )
```

profile of v0, /device:TPU:32, one launch (start us, length us, event | category | flops | bytes accessed | tf_op | source)
XLA Modules:
  0.0 202.2 jit_solution(12638515932917922644)
XLA Ops:
  0.6 75.5 %conditional.3 = (bf16[2,128,384]{2,1,0:T(8,128)(2,1)S(1)}, bf16[64,2,8,384]{3,2,1,0:T(8,128)(2,1)}, f32[512,1536]{1,0:T(8,128)}, bf16[512,1536]{1,0:T(8,128)(2,1)}, bf16[512,768]{1,0:T(8,128)(2,1)S(1)}) conditional(s32[]{:T(128)} %convert_element_type.2, (bf16[2,128,384]{2,1,0:T(8,128)(2,1)}, s32[2,128]{1,0:T(2,128)}, s32[2,128]{1,0:T(2,128)}, ...), branch_computations={%region_0.0_spmd, %region_1.0_spmd} | conditional | flops 2617245696 | bytes 17911960 | solution.py:456
  0.7 1.2 place.5
  1.9 41.3 %all_to_all.32 = bf16[128,8,384]{2,1,0:T(8,128)(2,1)} all-to-all(bf16[128,8,384]{2,1,0:T(8,128)(2,1)S(1)} %bitcast.31), channel_id=1, replica_groups=mesh['section'=2,'expert'=64,'head'=2] {'expert','head'}, dimensions={0} | all-to-all | bytes 1572864 | tf_op jit(solution)/shard_map/cond/branch_1_fun/all_to_all | solution.py:424
  43.2 7.9 %expert_forward.1 = (bf16[64,2,8,384]{3,2,1,0:T(8,128)(2,1)S(1)}, f32[512,1536]{1,0:T(8,128)}, bf16[512,1536]{1,0:T(8,128)(2,1)}, bf16[512,768]{1,0:T(8,128)(2,1)S(1)}) custom-call(bf16[64,2,8,384]{3,2,1,0:T(8,128)(2,1)} %bitcast.3.rows, f32[1,768]{1,0:T(1,128)} %get-tuple-element.101.gain, bf16[768,1536]{1,0:T(8,128)(2,1)} %get-tuple-element.102.w_in, ...), custom_call_target="tpu_custom_call" | custom-call | flops 2415919104 | bytes 11799552 | tf_op jit(solution)/shard_map/cond/branch_1_fun/expert_forward/pallas_call | solution.py:45
  51.1 24.7 %all_to_all.33 = bf16[128,8,384]{2,1,0:T(8,128)(2,1)S(1)} all-to-all(bf16[128,8,384]{2,1,0:T(8,128)(2,1)S(1)} %bitcast.35), channel_id=1, replica_groups=mesh['section'=2,'expert'=64,'head'=2] {'expert','head'}, dimensions={0} | all-to-all | bytes 1572864 | tf_op jit(solution)/shard_map/cond/branch_1_fun/all_to_all | solution.py:424
  75.7 0.0 copy-done.1
  75.7 0.0 copy-done.5
  75.7 0.0 copy-done.9
  75.7 0.4 gather.4
  76.2 0.1 collective-permute-start
  76.3 1.4 collective-permute-done
  77.7 10.3 %conditional.4 = (bf16[2,128,384]{2,1,0:T(8,128)(2,1)S(1)}, f32[512,1536]{1,0:T(8,128)}, bf16[64,2,8,384]{3,2,1,0:T(8,128)(2,1)}, bf16[512,1536]{1,0:T(8,128)(2,...) conditional(s32[]{:T(128)} %convert_element_type.2, (bf16[2,128,384]{2,1,0:T(8,128)(2,1)S(1)}, ...), branch_computations={%region_2.0_spmd, %region_3.0_spmd} | conditional | flops 3825205248 | bytes 32062656 | solution.py:471
  77.7 0.9 copy.26
  78.6 2.1 %copy.28 = bf16[64,2,8,384]{3,2,1,0:T(8,128)(2,1)} copy(bf16[64,2,8,384]{3,2,1,0:T(8,128)(2,1)} %get-tuple-element.202) | data formatting | bytes 1572864 | tf_op jit(solution)/shard_map/cond
  80.7 0.9 copy.31
  81.6 5.1 %multiply_add_fusion.1 = f32[512,1536]{1,0:T(8,128)} fusion(f32[512,1536]{1,0:T(8,128)} %get-tuple-element.122), kind=kLoop, calls=%fused_computation.3 | loop fusion | flops 11796480 | bytes 6291456 | tf_op jit(solution)/shard_map/cond/branch_1_fun/add | solution.py:31
  86.8 1.2 broadcast.20
  88.0 47.0 %collective-permute-start.1 = (bf16[2,128,384]{2,1,0:T(8,128)(2,1)S(1)}, bf16[2,128,384]{2,1,0:T(8,128)(2,1)S(1)}, u32[]{:S(2)}, u32[]{:S(2)}) collective-permute-start(bf16[2,128,384]{2,1,0:T(8,128)(2,1)S(1)} %get-tuple-element.179), channel_id=1, source_target_pairs={{0,128},{128,0},{1,129},{129,1},{2,130},{130,2},{3,131},{131,3},{4... | collective-permute-start | bytes 589832 | tf_op jit(solution)/shard_map/ppermute | solution.py:429
  135.1 1.1 collective-permute-done.1
  136.1 65.3 %conditional.5 = (bf16[768,1536]{1,0:T(8,128)(2,1)}, bf16[1536,768]{1,0:T(8,128)(2,1)}, bf16[1,2,128,384]{3,2,1,0:T(8,128)(2,1)S(1)}) conditional(s32[]{:T(128)} %convert_element_type.2, (bf16[512,768]{1,0:T(8,128)(2,1)}, bf16[512,1536]{1,0:T(8,128)(2,1)}, bf16[512,1536]{1,0:T(8,128)(2,1)}, bf16[512,768]{1,0:T(8,128)(2,1)}, ...), branch_computations={%region_4.0_spmd, %region_5.0_spmd} | conditional | flops 5033164800 | bytes 28131440 | solution.py:488
  136.1 1.2 place.7
  137.4 31.0 %all_to_all.35 = bf16[128,8,384]{2,1,0:T(8,128)(2,1)S(1)} all-to-all(bf16[128,8,384]{2,1,0:T(8,128)(2,1)S(1)} %bitcast.28), channel_id=1, replica_groups=mesh['section'=2,'expert'=64,'head'=2] {'expert','head'}, dimensions={0} | all-to-all | bytes 1572864 | tf_op jit(solution)/shard_map/cond/branch_1_fun/all_to_all | solution.py:424
  168.3 8.0 %expert_backward.1 = (bf16[64,2,8,384]{3,2,1,0:T(8,128)(2,1)}, bf16[512,1536]{1,0:T(8,128)(2,1)S(1)}, bf16[512,768]{1,0:T(8,128)(2,1)S(1)}) custom-call(bf16[64,2,8,384]{3,2,1,0:T(8,128)(2,1)S(1)} %bitcast.33, f32[512,1536]{1,0:T(8,128)} %get-tuple-element.142.slope, bf16[768,1536]{1,0:T(8,128)(2,1)} %get-tuple-element.143.w_in, ...), custom_call_target="tpu_custom_call" | custom-call | flops 2415919104 | bytes 12585984 | tf_op jit(solution)/shard_map/cond/branch_1_fun/expert_backward/pallas_call | solution.py:45
  176.4 6.3 %all-to-all-start.7 = ((bf16[128,8,384]{2,1,0:T(8,128)(2,1)}), bf16[128,8,384]{2,1,0:T(8,128)(2,1)S(1)}, u32[]{:S(2)}, u32[]{:S(2)}) async-start(bf16[128,8,384]{2,1,0:T(8,128)(2,1)} %bitcast.15), calls=%async_computation.7 | async-start | bytes 1572864 | tf_op jit(solution)/shard_map/cond/branch_1_fun/all_to_all | solution.py:424
  182.7 0.0 copy-start.8
  182.7 0.0 copy-start.12
  182.7 5.6 %weight_grads.3 = (bf16[768,1536]{1,0:T(8,128)(2,1)}, bf16[1536,768]{1,0:T(8,128)(2,1)}) custom-call(bf16[512,768]{1,0:T(8,128)(2,1)} %get-tuple-element.137.normed, bf16[512,1536]{1,0:T(8,128)(2,1)S(1)} %get-tuple-element.147.pre_grad, bf16[512,1536]{1,0:T(8,128)(2,1)} %get-tuple-element.148.act, bf16[512,768]{1,0:T(8,128)(2,1)S(1)} %get-tuple-element.149.flat), custom_call_target="tpu_custom_call" | custom-call | flops 2415919104 | bytes 9437184 | tf_op jit(solution)/shard_map/cond/branch_1_fun/weight_grads/pallas_call | solution.py:45
  188.4 12.6 %all-to-all-done.7 = bf16[128,8,384]{2,1,0:T(8,128)(2,1)S(1)} async-done(((bf16[128,8,384]{2,1,0:T(8,128)(2,1)}), bf16[128,8,384]{2,1,0:T(8,128)(2,1)S(1)}, u32[]{:S(2)}, u32[]{:S(2)}) %all-to-all-start.7) | async-done | bytes 786464 | tf_op jit(solution)/shard_map/cond/branch_1_fun/all_to_all | solution.py:424
  201.0 0.0 copy-done.8
  201.0 0.5 gather.7
  201.5 0.0 copy-start.4
  201.5 0.7 copy-done.4
  (10 shorter events, 0.0 us)
Async XLA Ops:
  43.2 32.6 %copy-start.1 = (bf16[2,128,384]{2,1,0:T(8,128)(2,1)S(1)}, bf16[2,128,384]{2,1,0:T(8,128)(2,1)}, u32[]{:S(2)}) copy-start(bf16[2,128,384]{2,1,0:T(8,128)(2,1)} %get-tuple-element.98.refs_0_.refs_4_) | copy-start | bytes 589828 | tf_op jit(solution)/shard_map/cond
  43.2 32.6 %copy-start.5 = (s32[2,128]{1,0:T(2,128)S(1)}, s32[2,128]{1,0:T(2,128)}, u32[]{:S(2)}) copy-start(s32[2,128]{1,0:T(2,128)} %get-tuple-element.99.refs_1_) | copy-start | bytes 3076 | tf_op jit(solution)/shard_map/cond
  43.2 32.6 %copy-start.9 = (s32[2,128]{1,0:T(2,128)S(1)}, s32[2,128]{1,0:T(2,128)}, u32[]{:S(2)}) copy-start(s32[2,128]{1,0:T(2,128)} %get-tuple-element.100.refs_2_) | copy-start | bytes 3076 | tf_op jit(solution)/shard_map/cond
  43.2 32.6 %copy-start.14 = (f32[2,128]{1,0:T(2,128)S(1)}, f32[2,128]{1,0:T(2,128)}, u32[]{:S(2)}) copy-start(f32[2,128]{1,0:T(2,128)} %get-tuple-element.105.refs_3_) | copy-start | bytes 3076 | tf_op jit(solution)/shard_map/cond
  76.2 1.5 copy-start.3
  76.2 1.5 collective-permute-start
  77.7 58.5 %copy-start.13 = (f32[1,2,128]{2,1,0:T(2,128)S(1)}, f32[1,2,128]{2,1,0:T(2,128)}, u32[]{:S(2)}) copy-start(f32[1,2,128]{2,1,0:T(2,128)} %param.15) | copy-start | bytes 3076
  88.0 48.1 %collective-permute-start.1 = (bf16[2,128,384]{2,1,0:T(8,128)(2,1)S(1)}, bf16[2,128,384]{2,1,0:T(8,128)(2,1)S(1)}, u32[]{:S(2)}, u32[]{:S(2)}) collective-permute-start(bf16[2,128,384]{2,1,0:T(8,128)(2,1)S(1)} %get-tuple-element.179), channel_id=1, source_target_pairs={{0,128},{128,0},{1,129},{129,1},{2,130},{130,2},{3,131},{131,3},{4... | collective-permute-start | bytes 589832 | tf_op jit(solution)/shard_map/ppermute | solution.py:429
  176.4 24.6 %all-to-all-start.7 = ((bf16[128,8,384]{2,1,0:T(8,128)(2,1)}), bf16[128,8,384]{2,1,0:T(8,128)(2,1)S(1)}, u32[]{:S(2)}, u32[]{:S(2)}) async-start(bf16[128,8,384]{2,1,0:T(8,128)(2,1)} %bitcast.15), calls=%async_computation.7 | async-start | bytes 1572864 | tf_op jit(solution)/shard_map/cond/branch_1_fun/all_to_all | solution.py:424
  182.7 18.3 %copy-start.8 = (s32[2,128]{1,0:T(2,128)S(1)}, s32[2,128]{1,0:T(2,128)}, u32[]{:S(2)}) copy-start(s32[2,128]{1,0:T(2,128)} %get-tuple-element.139.refs_1_) | copy-start | bytes 3076 | tf_op jit(solution)/shard_map/cond
  182.7 18.3 %copy-start.12 = (s32[2,128]{1,0:T(2,128)S(1)}, s32[2,128]{1,0:T(2,128)}, u32[]{:S(2)}) copy-start(s32[2,128]{1,0:T(2,128)} %get-tuple-element.140.refs_2_) | copy-start | bytes 3076 | tf_op jit(solution)/shard_map/cond
  201.5 0.7 copy-start.4
where the time goes:
time: 203 us; the launch traced here: 202 us
  blocking collectives  96.9 us (48%)
  starting transfers between devices  53.5 us (26%)
  Pallas kernels  24.9 us (12%)
  waiting for transfers between devices  15.1 us (7%)
  local copies, waits for them, and re-layouts  5.89 us (3%)
  other arithmetic  5.14 us (3%)
    all_to_all x3, blocking collectives, exchange(): lax.all_to_all(flat, ('expert', 'head'), 0, 0, tiled=True)  96.9 us
    ppermute x2, starting transfers between devices, swap(): lax.ppermute(block, 'section', [(i, (i + 1) % count) for i in range(count)])  47.1 us
    pallas_call x7, Pallas kernels, call(): pl.pallas_call(body, out_shape=outs, scratch_shapes=scratch, compiler_par...  24.9 us
    all_to_all x1, waiting for transfers between devices, exchange(): lax.all_to_all(flat, ('expert', 'head'), 0, 0, tiled=True)  12.6 us
    all_to_all x1, starting transfers between devices, exchange(): lax.all_to_all(flat, ('expert', 'head'), 0, 0, tiled=True)  6.33 us
    add x1, other arithmetic, act_and_slope(): up + 0.5 * v * (1.0 - th * th) * (ROOT_COEF + 3.0 * CUBE_COEF * ROOT_COEF...  5.14 us
  transfers between devices with their start and end apart: 3, of which 3 were waited for; matrix products, arithmetic and copies ran while one was open for 0% of the time, Pallas kernels for 3%

commit v1 on v0

v1 whole, which is shorter than its diff:
```python
import functools

import jax
import jax.numpy as jnp
from jax import lax
from jax.experimental import pallas as pl
from jax.experimental.pallas import tpu as pltpu
from jax.sharding import PartitionSpec as P

EPSILON = 1e-06
ROOT_COEF = 0.7978845608
CUBE_COEF = 0.044715
VMEM_LIMIT = 40 * 1024 * 1024
BF16, F32 = jnp.bfloat16, jnp.float32


def activate(v):
    sq = v * v
    th = jnp.tanh(ROOT_COEF * (v + CUBE_COEF * sq * v))
    up = 0.5 * (1.0 + th)
    return th, sq, up


def act_of(v):
    _, _, up = activate(v)
    return v * up


def act_and_slope(v):
    th, sq, up = activate(v)
    slope = up + 0.5 * v * (1.0 - th * th) * (ROOT_COEF + (3.0 * CUBE_COEF * ROOT_COEF) * sq)
    return v * up, slope


def dot(a, b, dims=((1,), (0,))):
    return lax.dot_general(a, b, (dims, ((), ())), preferred_element_type=F32)


def call(body, outs, ins, flops, grid=(), in_specs=None, out_specs=None, scratch=(), name=None):
    moved = sum(a.size * a.dtype.itemsize for a in ins)
    moved += sum(s.size * s.dtype.itemsize for s in outs)
    kwargs = {}
    if grid:
        kwargs = dict(grid=grid, in_specs=in_specs, out_specs=out_specs)
    return pl.pallas_call(
        body,
        out_shape=outs,
        scratch_shapes=scratch,
        compiler_params=pltpu.CompilerParams(vmem_limit_bytes=VMEM_LIMIT),
        cost_estimate=pl.CostEstimate(flops=flops, bytes_accessed=moved, transcendentals=0),
        name=name,
        **kwargs,
    )(*ins)


def struct(shape, dtype):
    return jax.ShapeDtypeStruct(shape, dtype)


def one_hot(ids, slots, experts, cap):
    micro, tokens = ids.shape
    per = micro * cap
    target = jnp.where(slots < cap, ids * per + slots, -1 - cap * micro)
    pieces = [target[m : m + 1] + m * cap for m in range(micro)]
    target = jnp.concatenate(pieces, axis=1)
    rows = lax.broadcasted_iota(jnp.int32, (experts * per, micro * tokens), 0)
    return (rows == target).astype(F32).astype(BF16)


def column(rows):
    flat = jnp.concatenate([rows[m : m + 1] for m in range(rows.shape[0])], axis=1)
    return jnp.transpose(jnp.broadcast_to(flat, (8, flat.shape[1])))[:, :1]


def place_body(scaled, cap, *refs):
    tok, ids, slots = refs[:3]
    outs = refs[4:] if scaled else refs[3:]
    prob = refs[3]
    experts, heads, per, _ = outs[0].shape
    tokens = tok[...].reshape(-1, tok.shape[2])
    if scaled:
        tokens = (column(prob[...]) * tokens.astype(F32)).astype(BF16)
    hot = one_hot(ids[...], slots[...], experts, cap)
    start = 0
    for out in outs:
        stop = start + out.shape[3]
        rows = dot(hot, tokens[:, start:stop]).reshape(experts, per, stop - start).astype(BF16)
        for h in range(heads):
            out[:, h] = rows
        start = stop


def place(tokens, ids, slots, prob, experts, cap, parts=None):
    micro, count, half = tokens.shape
    outs = [struct((experts, 2, micro * cap, part), BF16) for part in parts or (half,)]
    ins = (tokens, ids, slots) + (() if prob is None else (prob,))
    flops = 2 * experts * micro * cap * micro * count * half
    placed = call(functools.partial(place_body, prob is not None, cap), outs, ins, flops, name="place")
    return placed if parts else placed[0]


def gather_body(forward, cap, *refs):
    if forward:
        got, ids, slots, prob, base, out = refs
    else:
        got, ids, slots, base, out = refs
    experts, heads, per, half = got.shape
    hot = one_hot(ids[...], slots[...], experts, cap)
    first = got[:, 0].astype(F32).reshape(experts * per, half)
    second = got[:, 1].astype(F32).reshape(experts * per, half)
    if forward:
        picked = dot(hot, (first + second).astype(BF16), ((0,), (0,)))
        picked = column(prob[...]) * picked
    else:
        picked = dot(hot, first.astype(BF16), ((0,), (0,))) + dot(hot, second.astype(BF16), ((0,), (0,)))
    total = base[...].reshape(-1, half).astype(F32) + picked
    out[...] = total.astype(BF16).reshape(out.shape)


def gather(got, ids, slots, prob, base, cap):
    ins = (got, ids, slots) + (() if prob is None else (prob,)) + (base,)
    flops = 2 * got.shape[0] * got.shape[2] * base.size
    return call(
        functools.partial(gather_body, prob is not None, cap), [struct(base.shape, BF16)], ins, flops, name="gather"
    )[0]


def rows_of(ref):
    experts, heads, per, half = ref.shape
    return [ref[:, h].astype(F32).reshape(experts * per, half) for h in range(heads)]


def inverse(parts, width):
    total = sum(jnp.sum(v * v, axis=1, keepdims=True) for v in parts)
    return lax.rsqrt(total * (1.0 / width) + EPSILON)


def fill_normed(rows_ref, gain_ref, normed_ref):
    parts = rows_of(rows_ref)
    half = parts[0].shape[1]
    scale = inverse(parts, 2 * half)
    for h, v in enumerate(parts):
        cols = pl.ds(h * half, half)
        normed_ref[:, cols] = (v * scale * gain_ref[:, cols]).astype(BF16)


def spread(total, out_ref):
    experts, heads, per, half = out_ref.shape
    for h in range(heads):
        piece = total[:, h * half : (h + 1) * half]
        out_ref[:, h] = piece.reshape(experts, per, half).astype(BF16)


def spread_norm_grad(total, rows_ref, gain_ref, out_ref):
    experts, heads, per, half = out_ref.shape
    parts = rows_of(rows_ref)
    scale = inverse(parts, heads * half)
    grads = [total[:, h * half : (h + 1) * half] * gain_ref[:, pl.ds(h * half, half)] for h in range(heads)]
    cross = sum(jnp.sum(g * v, axis=1, keepdims=True) for g, v in zip(grads, parts))
    factor = scale * scale * scale * cross * (1.0 / (heads * half))
    for h in range(heads):
        piece = scale * grads[h] - parts[h] * factor
        out_ref[:, h] = piece.reshape(experts, per, half).astype(BF16)


def whole(shape):
    return pl.BlockSpec(shape, lambda j: (0,) * len(shape))


CHUNK = 256
GROUPS = 2


def sizes(rows, w_in):
    count = rows.shape[0] * rows.shape[2]
    width, hidden = w_in.shape
    return count, width, hidden


def expert_group(ref, r):
    step = ref.shape[0] // GROUPS
    return ref.at[pl.ds(r * step, step)]


def row_group(ref, r):
    step = ref.shape[0] // GROUPS
    return ref.at[pl.ds(pl.multiple_of(r * step, step), step)]


def over_groups(body):
    pl.loop(0, GROUPS)(body)


def copies_of(pairs, sems):
    return [pltpu.make_async_copy(src, dst, sems.at[i]) for i, (src, dst) in enumerate(pairs)]


def start_all(copies):
    for copy in copies:
        copy.start()


def flatten(grads, flat):
    half = grads.shape[3]
    for h, v in enumerate(rows_of(grads)):
        flat[:, pl.ds(h * half, half)] = v.astype(BF16)


def owned(body, outs, ins, flops, scratch, sems, name):
    moved = sum(a.size * a.dtype.itemsize for a in ins)
    moved += sum(s.size * s.dtype.itemsize for s in outs)
    return pl.pallas_call(
        body,
        out_shape=outs,
        in_specs=[
            pl.BlockSpec(memory_space=pltpu.VMEM if a.size < 4096 else pl.ANY) for a in ins
        ],
        out_specs=[pl.BlockSpec(memory_space=pl.ANY) for _ in outs],
        scratch_shapes=[pltpu.VMEM(shape, dtype) for shape, dtype in scratch] + [pltpu.SemaphoreType.DMA((sems,))],
        compiler_params=pltpu.CompilerParams(vmem_limit_bytes=VMEM_LIMIT),
        cost_estimate=pl.CostEstimate(flops=flops, bytes_accessed=moved, transcendentals=0),
        name=name,
    )(*ins)


def forward_body(rows, gain, w_in, w_out, out, rows_v, w_in_v, w_out_v, normed, out_v, sems):
    loads = copies_of([(rows, rows_v), (w_in, w_in_v), (w_out, w_out_v)], sems)
    start_all(loads)

    def stored(r):
        return pltpu.make_async_copy(expert_group(out_v, r), expert_group(out, r), sems.at[3 + r])

    loads[0].wait()

    @over_groups
    def _(r):
        fill_normed(expert_group(rows_v, r), gain, normed)

        @pl.when(r == 0)
        def _():
            loads[1].wait()

        act = act_of(dot(normed[...], w_in_v[...])).astype(BF16)

        @pl.when(r == 0)
        def _():
            loads[2].wait()

        spread(dot(act, w_out_v[...]), expert_group(out_v, r))
        stored(r).start()

    for r in range(GROUPS):
        stored(r).wait()


def expert_forward(rows, gain, w_in, w_out):
    count, width, hidden = sizes(rows, w_in)
    return owned(
        forward_body,
        [struct(rows.shape, BF16)],
        (rows, gain, w_in, w_out),
        4 * count * width * hidden,
        [
            (rows.shape, BF16),
            (w_in.shape, BF16),
            (w_out.shape, BF16),
            ((count // GROUPS, width), BF16),
            (rows.shape, BF16),
        ],
        3 + GROUPS,
        "expert_forward",
    )[0]


def grad_act_body(grads, w_out, out, flat):
    @pl.when(pl.program_id(0) == 0)
    def _():
        flatten(grads, flat)

    out[...] = dot(flat[...], w_out[...], ((1,), (1,)))


def grad_act_early(grads, w_out):
    hidden, width = w_out.shape
    count = grads.shape[0] * grads.shape[2]
    return call(
        grad_act_body,
        [struct((count, hidden), F32)],
        (grads, w_out),
        2 * count * width * hidden,
        grid=(hidden // CHUNK,),
        in_specs=[whole(grads.shape), pl.BlockSpec((CHUNK, width), lambda j: (j, 0))],
        out_specs=[pl.BlockSpec((count, CHUNK), lambda j: (0, j))],
        scratch=[pltpu.VMEM((count, width), BF16)],
        name="grad_act",
    )[0]


def slope_body(rows, gain, w_in, out, normed):
    @pl.when(pl.program_id(0) == 0)
    def _():
        fill_normed(rows, gain, normed)

    out[...] = act_and_slope(dot(normed[...], w_in[...]))[1]


def slope_of_rows(rows, gain, w_in):
    count, width, hidden = sizes(rows, w_in)
    return call(
        slope_body,
        [struct((count, hidden), F32)],
        (rows, gain, w_in),
        2 * count * width * hidden,
        grid=(hidden // CHUNK,),
        in_specs=[whole(rows.shape), whole(gain.shape), pl.BlockSpec((width, CHUNK), lambda j: (0, j))],
        out_specs=[pl.BlockSpec((count, CHUNK), lambda j: (0, j))],
        scratch=[pltpu.VMEM((count, width), BF16)],
        name="slope",
    )[0]


def both_body(rows, gain, w_in, grad_act, out, kept, rows_v, w_in_v, ga_v, normed, pre_grad, out_v, sems):
    loads = copies_of([(rows, rows_v), (w_in, w_in_v), (grad_act, ga_v)], sems)
    start_all(loads)

    def stored(r):
        return pltpu.make_async_copy(expert_group(out_v, r), expert_group(out, r), sems.at[3 + r])

    def saved(r):
        return pltpu.make_async_copy(row_group(pre_grad, r), row_group(kept, r), sems.at[3 + GROUPS + r])

    loads[0].wait()

    @over_groups
    def _(r):
        row = expert_group(rows_v, r)
        fill_normed(row, gain, normed)

        @pl.when(r == 0)
        def _():
            loads[1].wait()

        slope = act_and_slope(dot(normed[...], w_in_v[...]))[1]

        @pl.when(r == 0)
        def _():
            loads[2].wait()

        pre = (row_group(ga_v, r)[...] * slope).astype(BF16)
        row_group(pre_grad, r)[...] = pre
        saved(r).start()
        spread_norm_grad(dot(pre, w_in_v[...], ((1,), (1,))), row, gain, expert_group(out_v, r))
        stored(r).start()

    for r in range(GROUPS):
        stored(r).wait()
        saved(r).wait()


def expert_both(rows, gain, w_in, grad_act):
    count, width, hidden = sizes(rows, w_in)
    return owned(
        both_body,
        [struct(rows.shape, BF16), struct((count, hidden), BF16)],
        (rows, gain, w_in, grad_act),
        4 * count * width * hidden,
        [
            (rows.shape, BF16),
            (w_in.shape, BF16),
            ((count, hidden), F32),
            ((count // GROUPS, width), BF16),
            ((count, hidden), BF16),
            (rows.shape, BF16),
        ],
        3 + 2 * GROUPS,
        "expert_both",
    )


def backward_body(
    grads, slope, w_in, w_out, rows, gain, out, kept, grads_v, slope_v, w_in_v, w_out_v, rows_v, flat, pre_grad, out_v, sems
):
    pairs = [(grads, grads_v), (w_out, w_out_v), (slope, slope_v), (w_in, w_in_v), (rows, rows_v)]
    loads = copies_of(pairs, sems)
    start_all(loads)

    def stored(r):
        return pltpu.make_async_copy(expert_group(out_v, r), expert_group(out, r), sems.at[5 + r])

    def saved(r):
        return pltpu.make_async_copy(row_group(pre_grad, r), row_group(kept, r), sems.at[5 + GROUPS + r])

    loads[0].wait()

    @over_groups
    def _(r):
        flatten(expert_group(grads_v, r), flat)

        @pl.when(r == 0)
        def _():
            loads[1].wait()

        grad_act = dot(flat[...], w_out_v[...], ((1,), (1,)))

        @pl.when(r == 0)
        def _():
            loads[2].wait()

        pre = (grad_act * row_group(slope_v, r)[...]).astype(BF16)
        row_group(pre_grad, r)[...] = pre
        saved(r).start()

        @pl.when(r == 0)
        def _():
            loads[3].wait()
            loads[4].wait()

        total = dot(pre, w_in_v[...], ((1,), (1,)))
        spread_norm_grad(total, expert_group(rows_v, r), gain, expert_group(out_v, r))
        stored(r).start()

    for r in range(GROUPS):
        stored(r).wait()
        saved(r).wait()


def expert_backward(grads, slope, w_in, w_out, rows, gain):
    count, width, hidden = sizes(rows, w_in)
    return owned(
        backward_body,
        [struct(rows.shape, BF16), struct((count, hidden), BF16)],
        (grads, slope, w_in, w_out, rows, gain),
        4 * count * width * hidden,
        [
            (grads.shape, BF16),
            (slope.shape, F32),
            (w_in.shape, BF16),
            (w_out.shape, BF16),
            (rows.shape, BF16),
            ((count // GROUPS, width), BF16),
            ((count, hidden), BF16),
            (rows.shape, BF16),
        ],
        5 + 2 * GROUPS,
        "expert_backward",
    )


def weight_grad_body(rows, gain, grads, w_in, pre_grad, first, second, normed, flat):
    @pl.when(pl.program_id(0) == 0)
    def _():
        fill_normed(rows, gain, normed)
        flatten(grads, flat)

    first[...] = dot(normed[...], pre_grad[...], ((0,), (0,))).astype(BF16)
    act = act_of(dot(normed[...], w_in[...])).astype(BF16)
    second[...] = dot(act, flat[...], ((0,), (0,))).astype(BF16)


def weight_grads(rows, gain, grads, w_in, pre_grad):
    count, width, hidden = sizes(rows, w_in)
    columns = pl.BlockSpec((width, CHUNK), lambda j: (0, j))
    return call(
        weight_grad_body,
        [struct((width, hidden), BF16), struct((hidden, width), BF16)],
        (rows, gain, grads, w_in, pre_grad),
        6 * count * width * hidden,
        grid=(hidden // CHUNK,),
        in_specs=[
            whole(rows.shape),
            whole(gain.shape),
            whole(grads.shape),
            columns,
            pl.BlockSpec((count, CHUNK), lambda j: (0, j)),
        ],
        out_specs=[columns, pl.BlockSpec((CHUNK, width), lambda j: (j, 0))],
        scratch=[pltpu.VMEM((count, width), BF16), pltpu.VMEM((count, width), BF16)],
        name="weight_grads",
    )


def exchange(blocks):
    experts, heads, per, part = blocks.shape
    flat = blocks.reshape(experts * heads, per, part)
    return lax.all_to_all(flat, ("expert", "head"), 0, 0, tiled=True).reshape(blocks.shape)


def swap(block):
    count = lax.axis_size("section")
    return lax.ppermute(block, "section", [(i, (i + 1) % count) for i in range(count)])


def on_device(boundary, norm_gain, gate_prob, expert_ids, slot_ids, weight_in, weight_out):
    experts = lax.axis_size("expert")
    local = boundary[0]
    micro, count, half = local.shape
    cap = 2 * count // experts
    w_in = weight_in[0, 0]
    w_out = weight_out[0, 0]
    ids, slots, prob = expert_ids[0], slot_ids[0], gate_prob[0]
    first = lax.axis_index("section") == 0

    def stage_one_lower():
        rows = exchange(place(local, ids, slots, None, experts, cap))
        part = expert_forward(rows, norm_gain, w_in, w_out)
        return gather(exchange(part), ids, slots, prob, local, cap), rows

    def stage_one_upper():
        small, large = place(local, ids, slots, prob, experts, cap, (half // 3, half - half // 3))
        small, large = lax.optimization_barrier((exchange(small), large))
        return local, jnp.concatenate([small, exchange(large)], axis=3)

    sent, rows_one = lax.cond(first, stage_one_lower, stage_one_upper)
    hid = swap(sent)

    def stage_two_lower():
        slope = slope_of_rows(rows_one, norm_gain, w_in)
        return local, slope, rows_one, jnp.zeros(slope.shape, BF16)

    def stage_two_upper():
        rows = exchange(place(hid, ids, slots, None, experts, cap))
        grad_act = grad_act_early(rows_one, w_out)
        back, pre_grad = expert_both(rows, norm_gain, w_in, grad_act)
        grad_hid = gather(exchange(back), ids, slots, None, local, cap)
        return grad_hid, grad_act, rows, pre_grad

    sent, wide, rows_two, pre_grad = lax.cond(first, stage_two_lower, stage_two_upper)
    grad_hid = swap(sent)

    def stage_three_lower():
        grads = exchange(place(grad_hid, ids, slots, prob, experts, cap))
        back, pre_grad_low = expert_backward(grads, wide, w_in, w_out, rows_one, norm_gain)
        got = exchange(back)
        first_grad, second_grad = weight_grads(rows_one, norm_gain, grads, w_in, pre_grad_low)
        return gather(got, ids, slots, None, grad_hid, cap), first_grad, second_grad

    def stage_three_upper():
        part = expert_forward(rows_two, norm_gain, w_in, w_out)
        first_grad, second_grad = weight_grads(rows_two, norm_gain, rows_one, w_in, pre_grad)
        part, first_grad, second_grad = lax.optimization_barrier((part, first_grad, second_grad))
        return gather(exchange(part), ids, slots, prob, hid, cap), first_grad, second_grad

    result, first_grad, second_grad = lax.cond(first, stage_three_lower, stage_three_upper)
    return result[None], first_grad[None, None], second_grad[None, None]


def solution(mesh):
    placed = (
        P("section", None, "expert", "head"),
        P("section", None),
        P("section", None, "expert"),
        P("section", None, "expert"),
        P("section", None, "expert"),
        P("section", "expert", None, "head"),
        P("section", "expert", "head", None),
    )
    return jax.shard_map(
        on_device,
        mesh=mesh,
        in_specs=placed,
        out_specs=(
            P("section", None, "expert", "head"),
            P("section", "expert", None, "head"),
            P("section", "expert", "head", None),
        ),
        check_vma=False,
    )
```

time: 203 us -> 189 us (0.931)
  blocking collectives: 96.9 us -> 84.3 us
  Pallas kernels: 24.9 us -> 33.5 us
  other arithmetic: 5.14 us -> 0 us
  waiting for transfers between devices: 15.1 us -> 11.6 us
  local copies, waits for them, and re-layouts: 5.89 us -> 2.66 us
    pallas_call x0 -> x2, Pallas kernels: none -> 13.8 us  [owned(): pl.pallas_call(body, out_shape=outs, in_specs=[pl.BlockSpec(memory_space=...]
    all_to_all x3, blocking collectives: 96.9 us -> 84.3 us  [exchange(): lax.all_to_all(flat, ('expert', 'head'), 0, 0, tiled=True)]
    pallas_call x7 -> x6, Pallas kernels: 24.9 us -> 19.7 us  [call(): pl.pallas_call(body, out_shape=outs, scratch_shapes=scratch, compiler_par...]
    add x1 -> x0, other arithmetic: 5.14 us -> none  [act_and_slope(): up + 0.5 * v * (1.0 - th * th) * (ROOT_COEF + 3.0 * CUBE_COEF * ROOT_COEF...]
    all_to_all x1, waiting for transfers between devices: 12.6 us -> 9.13 us  [exchange(): lax.all_to_all(flat, ('expert', 'head'), 0, 0, tiled=True)]
    cond x15 -> x28, local copies, waits for them, and re-layouts: 3.97 us -> 1.88 us
  transfers between devices with their start and end apart: 3 -> 3, of which waited for: 3 -> 3; matrix products, arithmetic and copies ran while one was open for 0% -> 0% of each run, Pallas kernels for 3% -> 5%
where the time goes in v1:
time: 189 us
  blocking collectives  84.3 us (45%)
  starting transfers between devices  55.5 us (29%)
  Pallas kernels  33.5 us (18%)
  waiting for transfers between devices  11.6 us (6%)
  local copies, waits for them, and re-layouts  2.66 us (1%)
    all_to_all x3, blocking collectives, exchange(): lax.all_to_all(flat, ('expert', 'head'), 0, 0, tiled=True)  84.3 us
    ppermute x2, starting transfers between devices, swap(): lax.ppermute(block, 'section', [(i, (i + 1) % count) for i in range(count)])  49.1 us
    pallas_call x6, Pallas kernels, call(): pl.pallas_call(body, out_shape=outs, scratch_shapes=scratch, compiler_par...  19.7 us
    pallas_call x2, Pallas kernels, owned(): pl.pallas_call(body, out_shape=outs, in_specs=[pl.BlockSpec(memory_space=...  13.8 us
    all_to_all x1, waiting for transfers between devices, exchange(): lax.all_to_all(flat, ('expert', 'head'), 0, 0, tiled=True)  9.13 us
    all_to_all x1, starting transfers between devices, exchange(): lax.all_to_all(flat, ('expert', 'head'), 0, 0, tiled=True)  6.34 us
  transfers between devices with their start and end apart: 3, of which 3 were waited for; matrix products, arithmetic and copies ran while one was open for 0% of the time, Pallas kernels for 5%

profile of v1, /device:TPU:32, one launch (start us, length us, event | category | flops | bytes accessed | tf_op | source)
XLA Modules:
  0.0 188.7 jit_solution(15419223550071897255)
XLA Ops:
  0.6 68.5 %conditional.3 = (bf16[2,128,384]{2,1,0:T(8,128)(2,1)S(1)}, bf16[64,2,8,384]{3,2,1,0:T(8,128)(2,1)S(1)}) conditional(s32[]{:T(128)} %convert_element_type.2, (bf16[2,128,384]{2,1,0:T(8,128)(2,1)}, s32[2,128]{1,0:T(2,128)}, s32[2,128]{1,0:T(2,128)}, f32[2,128]{1,0:T(2,128)}) %tuple.72, (bf16[2,128,384]{2,1,0:T(8,128)(2,1)}, s32[2,128]{1,0:T(2,128)}, ...), branch_computations={%region_0.0_spmd, %region_1.0_spmd} | conditional | flops 2617245696 | bytes 28147952 | solution.py:513
  0.7 0.0 copy-start.3
  0.7 0.0 copy-start.18
  0.7 1.4 place.5
  2.1 35.3 %all_to_all.37 = bf16[128,8,384]{2,1,0:T(8,128)(2,1)S(1)} all-to-all(bf16[128,8,384]{2,1,0:T(8,128)(2,1)S(1)} %bitcast.33), channel_id=1, replica_groups=mesh['section'=2,'expert'=64,'head'=2] {'expert','head'}, dimensions={0} | all-to-all | bytes 1572864 | tf_op jit(solution)/shard_map/cond/branch_1_fun/all_to_all | solution.py:485
  37.4 0.0 copy-start.10
  37.4 0.0 copy-start.14
  37.4 0.0 copy-start.23
  37.5 6.6 %expert_forward.2 = bf16[64,2,8,384]{3,2,1,0:T(8,128)(2,1)S(1)} custom-call(bf16[64,2,8,384]{3,2,1,0:T(8,128)(2,1)S(1)} %bitcast.40, f32[1,768]{1,0:T(1,128)S(1)} %copy-done.18, bf16[768,1536]{1,0:T(8,128)(2,1)} %get-tuple-element.97.w_in, bf16[1536,768]{1,0:T(8,128)(2,1)S(1)} %copy-done.3), custom_call_target="tpu_custom_call" | custom-call | flops 2415919104 | bytes 6294528 | tf_op jit(solution)/shard_map/cond/branch_1_fun/expert_forward/pallas_call | solution.py:212
  44.1 24.6 %all_to_all.38 = bf16[128,8,384]{2,1,0:T(8,128)(2,1)S(1)} all-to-all(bf16[128,8,384]{2,1,0:T(8,128)(2,1)S(1)} %bitcast.38), channel_id=1, replica_groups=mesh['section'=2,'expert'=64,'head'=2] {'expert','head'}, dimensions={0} | all-to-all | bytes 1572864 | tf_op jit(solution)/shard_map/cond/branch_1_fun/all_to_all | solution.py:485
  68.7 0.4 gather.4
  69.1 0.1 collective-permute-start
  69.2 1.4 collective-permute-done
  70.6 8.8 %conditional.4 = (bf16[2,128,384]{2,1,0:T(8,128)(2,1)S(1)}, f32[512,1536]{1,0:T(8,128)}, bf16[64,2,8,384]{3,2,1,0:T(8,128)(2,1)}, bf16[512,1536]{1,0:T(8,128)(2,1)S(1)}) conditional(s32[]{:T(128)} %convert_element_type.2, (bf16[2,128,384]{2,1,0:T(8,128)(2,1)S(1)}, s32[2,128]{1,0:T(2,128)}, s32[2,128]{1,0:T(2,128)}, ...), branch_computations={%region_2.0_spmd, %region_3.0_spmd} | conditional | flops 3825205248 | bytes 31288524 | solution.py:527
  70.6 0.9 copy.18
  71.6 0.9 copy.20
  72.5 6.9 %slope.1 = f32[512,1536]{1,0:T(8,128)} custom-call(bf16[64,2,8,384]{3,2,1,0:T(8,128)(2,1)S(1)} %get-tuple-element.173.rows, f32[1,768]{1,0:T(1,128)} %get-tuple-element.112.gain, bf16[768,1536]{1,0:T(8,128)(2,1)} %get-tuple-element.113.w_in), custom_call_target="tpu_custom_call" | custom-call | flops 1207959552 | bytes 6294528 | tf_op jit(solution)/shard_map/cond/branch_1_fun/slope/pallas_call | solution.py:45
  79.3 0.1 broadcast.2
  79.4 49.0 %collective-permute-start.1 = (bf16[2,128,384]{2,1,0:T(8,128)(2,1)S(1)}, bf16[2,128,384]{2,1,0:T(8,128)(2,1)S(1)}, u32[]{:S(2)}, u32[]{:S(2)}) collective-permute-start(bf16[2,128,384]{2,1,0:T(8,128)(2,1)S(1)} %get-tuple-element.158), channel_id=1, source_target_pairs={{0,128},{128,0},{1,129},{129,1},{2,130},{130,2},{3,131},{131,3},{4... | collective-permute-start | bytes 589832 | tf_op jit(solution)/shard_map/ppermute | solution.py:490
  128.5 1.1 collective-permute-done.1
  129.5 58.5 %conditional.5 = (bf16[768,1536]{1,0:T(8,128)(2,1)}, bf16[1536,768]{1,0:T(8,128)(2,1)}, bf16[1,2,128,384]{3,2,1,0:T(8,128)(2,1)S(1)}) conditional(s32[]{:T(128)} %convert_element_type.2, (bf16[64,2,8,384]{3,2,1,0:T(8,128)(2,1)}, f32[1,768]{1,0:T(1,128)}, bf16[768,1536]{1,0:T(8,128)(2,1)}, bf16[1536,768]{1,0:T(8,128)(2,1)}, ...), branch_computations={%region_4.0_spmd, %region_5.0_spmd} | conditional | flops 6241124352 | bytes 40729796 | solution.py:543
  129.5 1.4 place.7
  131.0 24.4 %all_to_all.41 = bf16[128,8,384]{2,1,0:T(8,128)(2,1)S(1)} all-to-all(bf16[128,8,384]{2,1,0:T(8,128)(2,1)S(1)} %bitcast.30), channel_id=1, replica_groups=mesh['section'=2,'expert'=64,'head'=2] {'expert','head'}, dimensions={0} | all-to-all | bytes 1572864 | tf_op jit(solution)/shard_map/cond/branch_1_fun/all_to_all | solution.py:485
  155.4 7.1 %expert_backward.1 = (bf16[64,2,8,384]{3,2,1,0:T(8,128)(2,1)}, bf16[512,1536]{1,0:T(8,128)(2,1)S(1)}) custom-call(bf16[64,2,8,384]{3,2,1,0:T(8,128)(2,1)S(1)} %bitcast.34, f32[512,1536]{1,0:T(8,128)} %get-tuple-element.136.slope, bf16[768,1536]{1,0:T(8,128)(2,1)} %get-tuple-element.135.w_in, bf16[1536,768]{1,0:T(8,128)(2,1)S(1)} %copy-done.5, ...), custom_call_target="tpu_custom_call" | custom-call | flops 2415919104 | bytes 11799552 | tf_op jit(solution)/shard_map/cond/branch_1_fun/expert_backward/pallas_call | solution.py:212
  162.6 6.3 %all-to-all-start.6 = ((bf16[128,8,384]{2,1,0:T(8,128)(2,1)}), bf16[128,8,384]{2,1,0:T(8,128)(2,1)S(1)}, u32[]{:S(2)}, u32[]{:S(2)}) async-start(bf16[128,8,384]{2,1,0:T(8,128)(2,1)} %bitcast.17), calls=%async_computation.6 | async-start | bytes 1572864 | tf_op jit(solution)/shard_map/cond/branch_1_fun/all_to_all | solution.py:485
  168.9 0.0 copy-start.13
  169.0 0.0 copy-start.17
  169.0 9.2 %weight_grads.3 = (bf16[768,1536]{1,0:T(8,128)(2,1)}, bf16[1536,768]{1,0:T(8,128)(2,1)}) custom-call(bf16[64,2,8,384]{3,2,1,0:T(8,128)(2,1)} %copy-done.2, f32[1,768]{1,0:T(1,128)S(1)} %copy-done.21, bf16[64,2,8,384]{3,2,1,0:T(8,128)(2,1)S(1)} %bitcast.35, bf16[768,1536]{1,0:T(8,128)(2,1)} %get-tuple-element.135.w_in, ...), custom_call_target="tpu_custom_call" | custom-call | flops 3623878656 | bytes 10226688 | tf_op jit(solution)/shard_map/cond/branch_1_fun/weight_grads/pallas_call | solution.py:45
  178.1 9.1 %all-to-all-done.6 = bf16[128,8,384]{2,1,0:T(8,128)(2,1)S(1)} async-done(((bf16[128,8,384]{2,1,0:T(8,128)(2,1)}), bf16[128,8,384]{2,1,0:T(8,128)(2,1)S(1)}, u32[]{:S(2)}, u32[]{:S(2)}) %all-to-all-start.6) | async-done | bytes 786464 | tf_op jit(solution)/shard_map/cond/branch_1_fun/all_to_all | solution.py:485
  187.3 0.5 gather.7
  188.0 0.0 copy-start.9
  188.0 0.7 copy-done.9
  (21 shorter events, 0.0 us)
Async XLA Ops:
  0.7 36.8 %copy-start.3 = (bf16[1536,768]{1,0:T(8,128)(2,1)S(1)}, bf16[1536,768]{1,0:T(8,128)(2,1)}, u32[]{:S(2)}) copy-start(bf16[1536,768]{1,0:T(8,128)(2,1)} %get-tuple-element.98.w_out) | copy-start | bytes 7077892 | tf_op jit(solution)/shard_map/cond
  0.7 36.7 %copy-start.18 = (f32[1,768]{1,0:T(1,128)S(1)}, f32[1,768]{1,0:T(1,128)}, u32[]{:S(2)}) copy-start(f32[1,768]{1,0:T(1,128)} %get-tuple-element.96.gain) | copy-start | bytes 9220 | tf_op jit(solution)/shard_map/cond
  37.4 6.7 %copy-start = (bf16[128,8,384]{2,1,0:T(8,128)(2,1)}, bf16[128,8,384]{2,1,0:T(8,128)(2,1)S(1)}, u32[]{:S(2)}) copy-start(bf16[128,8,384]{2,1,0:T(8,128)(2,1)S(1)} %all_to_all.37) | copy-start | bytes 2359300 | tf_op jit(solution)/shard_map/cond
  37.4 31.3 %copy-start.7 = (bf16[2,128,384]{2,1,0:T(8,128)(2,1)S(1)}, bf16[2,128,384]{2,1,0:T(8,128)(2,1)}, u32[]{:S(2)}) copy-start(bf16[2,128,384]{2,1,0:T(8,128)(2,1)} %get-tuple-element.93.refs_0_.refs_4_) | copy-start | bytes 589828 | tf_op jit(solution)/shard_map/cond
  37.4 31.3 %copy-start.10 = (s32[2,128]{1,0:T(2,128)S(1)}, s32[2,128]{1,0:T(2,128)}, u32[]{:S(2)}) copy-start(s32[2,128]{1,0:T(2,128)} %get-tuple-element.94.refs_1_) | copy-start | bytes 3076 | tf_op jit(solution)/shard_map/cond
  37.4 31.3 %copy-start.14 = (s32[2,128]{1,0:T(2,128)S(1)}, s32[2,128]{1,0:T(2,128)}, u32[]{:S(2)}) copy-start(s32[2,128]{1,0:T(2,128)} %get-tuple-element.95.refs_2_) | copy-start | bytes 3076 | tf_op jit(solution)/shard_map/cond
  37.4 31.2 %copy-start.23 = (f32[2,128]{1,0:T(2,128)S(1)}, f32[2,128]{1,0:T(2,128)}, u32[]{:S(2)}) copy-start(f32[2,128]{1,0:T(2,128)} %get-tuple-element.99.refs_3_) | copy-start | bytes 3076 | tf_op jit(solution)/shard_map/cond
  44.1 25.0 %copy-start.1 = (bf16[128,8,384]{2,1,0:T(8,128)(2,1)S(1)}, bf16[128,8,384]{2,1,0:T(8,128)(2,1)}, u32[]{:S(2)}) copy-start(bf16[128,8,384]{2,1,0:T(8,128)(2,1)} %copy-done) | copy-start | bytes 2359300 | tf_op jit(solution)/shard_map/cond
  69.1 1.5 collective-permute-start
  70.6 58.9 %copy-start.22 = (f32[1,2,128]{2,1,0:T(2,128)S(1)}, f32[1,2,128]{2,1,0:T(2,128)}, u32[]{:S(2)}) copy-start(f32[1,2,128]{2,1,0:T(2,128)} %param.15) | copy-start | bytes 3076
  79.4 50.1 %collective-permute-start.1 = (bf16[2,128,384]{2,1,0:T(8,128)(2,1)S(1)}, bf16[2,128,384]{2,1,0:T(8,128)(2,1)S(1)}, u32[]{:S(2)}, u32[]{:S(2)}) collective-permute-start(bf16[2,128,384]{2,1,0:T(8,128)(2,1)S(1)} %get-tuple-element.158), channel_id=1, source_target_pairs={{0,128},{128,0},{1,129},{129,1},{2,130},{130,2},{3,131},{131,3},{4... | collective-permute-start | bytes 589832 | tf_op jit(solution)/shard_map/ppermute | solution.py:490
  129.5 33.1 %copy-start.2 = (bf16[64,2,8,384]{3,2,1,0:T(8,128)(2,1)}, bf16[64,2,8,384]{3,2,1,0:T(8,128)(2,1)S(1)}, u32[]{:S(2)}) copy-start(bf16[64,2,8,384]{3,2,1,0:T(8,128)(2,1)S(1)} %get-tuple-element.129.rows) | copy-start | bytes 2359300 | tf_op jit(solution)/shard_map/cond
  129.5 25.9 %copy-start.5 = (bf16[1536,768]{1,0:T(8,128)(2,1)S(1)}, bf16[1536,768]{1,0:T(8,128)(2,1)}, u32[]{:S(2)}) copy-start(bf16[1536,768]{1,0:T(8,128)(2,1)} %get-tuple-element.137.w_out) | copy-start | bytes 7077892 | tf_op jit(solution)/shard_map/cond
  129.5 25.9 %copy-start.21 = (f32[1,768]{1,0:T(1,128)S(1)}, f32[1,768]{1,0:T(1,128)}, u32[]{:S(2)}) copy-start(f32[1,768]{1,0:T(1,128)} %get-tuple-element.130.gain) | copy-start | bytes 9220 | tf_op jit(solution)/shard_map/cond
  162.6 24.7 %all-to-all-start.6 = ((bf16[128,8,384]{2,1,0:T(8,128)(2,1)}), bf16[128,8,384]{2,1,0:T(8,128)(2,1)S(1)}, u32[]{:S(2)}, u32[]{:S(2)}) async-start(bf16[128,8,384]{2,1,0:T(8,128)(2,1)} %bitcast.17), calls=%async_computation.6 | async-start | bytes 1572864 | tf_op jit(solution)/shard_map/cond/branch_1_fun/all_to_all | solution.py:485
  168.9 18.3 %copy-start.13 = (s32[2,128]{1,0:T(2,128)S(1)}, s32[2,128]{1,0:T(2,128)}, u32[]{:S(2)}) copy-start(s32[2,128]{1,0:T(2,128)} %get-tuple-element.132.refs_1_) | copy-start | bytes 3076 | tf_op jit(solution)/shard_map/cond
  169.0 18.3 %copy-start.17 = (s32[2,128]{1,0:T(2,128)S(1)}, s32[2,128]{1,0:T(2,128)}, u32[]{:S(2)}) copy-start(s32[2,128]{1,0:T(2,128)} %get-tuple-element.133.refs_2_) | copy-start | bytes 3076 | tf_op jit(solution)/shard_map/cond
  188.0 0.7 copy-start.9

commit v2 on v1

--- a/solution.py
+++ b/solution.py
@@ -10,7 +10,7 @@
 EPSILON = 1e-06
 ROOT_COEF = 0.7978845608
 CUBE_COEF = 0.044715
-VMEM_LIMIT = 40 * 1024 * 1024
+VMEM_LIMIT = 24 * 1024 * 1024
 BF16, F32 = jnp.bfloat16, jnp.float32
 
 
@@ -168,6 +168,7 @@
 
 
 CHUNK = 256
+NARROW = 128
 GROUPS = 2
 
 
@@ -288,9 +289,9 @@
         [struct((count, hidden), F32)],
         (grads, w_out),
         2 * count * width * hidden,
-        grid=(hidden // CHUNK,),
-        in_specs=[whole(grads.shape), pl.BlockSpec((CHUNK, width), lambda j: (j, 0))],
-        out_specs=[pl.BlockSpec((count, CHUNK), lambda j: (0, j))],
+        grid=(hidden // NARROW,),
+        in_specs=[whole(grads.shape), pl.BlockSpec((NARROW, width), lambda j: (j, 0))],
+        out_specs=[pl.BlockSpec((count, NARROW), lambda j: (0, j))],
         scratch=[pltpu.VMEM((count, width), BF16)],
         name="grad_act",
     )[0]
@@ -311,9 +312,9 @@
         [struct((count, hidden), F32)],
         (rows, gain, w_in),
         2 * count * width * hidden,
-        grid=(hidden // CHUNK,),
-        in_specs=[whole(rows.shape), whole(gain.shape), pl.BlockSpec((width, CHUNK), lambda j: (0, j))],
-        out_specs=[pl.BlockSpec((count, CHUNK), lambda j: (0, j))],
+        grid=(hidden // NARROW,),
+        in_specs=[whole(rows.shape), whole(gain.shape), pl.BlockSpec((width, NARROW), lambda j: (0, j))],
+        out_specs=[pl.BlockSpec((count, NARROW), lambda j: (0, j))],
         scratch=[pltpu.VMEM((count, width), BF16)],
         name="slope",
     )[0]
@@ -392,26 +393,22 @@
 
     loads[0].wait()
 
-    @over_groups
-    def _(r):
+    for r in range(GROUPS):
         flatten(expert_group(grads_v, r), flat)
 
-        @pl.when(r == 0)
-        def _():
+        if r == 0:
             loads[1].wait()
 
         grad_act = dot(flat[...], w_out_v[...], ((1,), (1,)))
 
-        @pl.when(r == 0)
-        def _():
+        if r == 0:
             loads[2].wait()
 
         pre = (grad_act * row_group(slope_v, r)[...]).astype(BF16)
         row_group(pre_grad, r)[...] = pre
         saved(r).start()
 
-        @pl.when(r == 0)
-        def _():
+        if r == 0:
             loads[3].wait()
             loads[4].wait()
 

time: 189 us -> 189 us (level)
  starting transfers between devices: 55.5 us -> 52.3 us
  Pallas kernels: 33.5 us -> 36.1 us
    ppermute x2, starting transfers between devices: 49.1 us -> 45.7 us  [swap(): lax.ppermute(block, 'section', [(i, (i + 1) % count) for i in range(count)])]
    pallas_call x6, Pallas kernels: 19.7 us -> 23.1 us  [call(): pl.pallas_call(body, out_shape=outs, scratch_shapes=scratch, compiler_par...]
where the time goes in v2:
time: 189 us; the launch traced here: 188 us
  blocking collectives  84.3 us (45%)
  starting transfers between devices  52.3 us (28%)
  Pallas kernels  36.1 us (19%)
  waiting for transfers between devices  11.6 us (6%)
  local copies, waits for them, and re-layouts  2.66 us (1%)
    all_to_all x3, blocking collectives, exchange(): lax.all_to_all(flat, ('expert', 'head'), 0, 0, tiled=True)  84.3 us
    ppermute x2, starting transfers between devices, swap(): lax.ppermute(block, 'section', [(i, (i + 1) % count) for i in range(count)])  45.7 us
    pallas_call x6, Pallas kernels, call(): pl.pallas_call(body, out_shape=outs, scratch_shapes=scratch, compiler_par...  23.1 us
    pallas_call x2, Pallas kernels, owned(): pl.pallas_call(body, out_shape=outs, in_specs=[pl.BlockSpec(memory_space=...  12.9 us
    all_to_all x1, waiting for transfers between devices, exchange(): lax.all_to_all(flat, ('expert', 'head'), 0, 0, tiled=True)  9.13 us
    all_to_all x1, starting transfers between devices, exchange(): lax.all_to_all(flat, ('expert', 'head'), 0, 0, tiled=True)  6.6 us
  transfers between devices with their start and end apart: 3, of which 3 were waited for; matrix products, arithmetic and copies ran while one was open for 0% of the time, Pallas kernels for 5%

profile of v2, /device:TPU:32, one launch (start us, length us, event | category | flops | bytes accessed | tf_op | source)
XLA Modules:
  0.0 188.1 jit_solution(16808753181596246343)
XLA Ops:
  0.6 68.5 %conditional.3 = (bf16[2,128,384]{2,1,0:T(8,128)(2,1)S(1)}, bf16[64,2,8,384]{3,2,1,0:T(8,128)(2,1)S(1)}) conditional(s32[]{:T(128)} %convert_element_type.2, (bf16[2,128,384]{2,1,0:T(8,128)(2,1)}, s32[2,128]{1,0:T(2,128)}, s32[2,128]{1,0:T(2,128)}, f32[2,128]{1,0:T(2,128)}) %tuple.72, (bf16[2,128,384]{2,1,0:T(8,128)(2,1)}, s32[2,128]{1,0:T(2,128)}, ...), branch_computations={%region_0.0_spmd, %region_1.0_spmd} | conditional | flops 2617245696 | bytes 28147952 | solution.py:510
  0.7 0.0 copy-start.3
  0.7 0.0 copy-start.18
  0.7 1.4 place.5
  2.1 35.3 %all_to_all.37 = bf16[128,8,384]{2,1,0:T(8,128)(2,1)S(1)} all-to-all(bf16[128,8,384]{2,1,0:T(8,128)(2,1)S(1)} %bitcast.33), channel_id=1, replica_groups=mesh['section'=2,'expert'=64,'head'=2] {'expert','head'}, dimensions={0} | all-to-all | bytes 1572864 | tf_op jit(solution)/shard_map/cond/branch_1_fun/all_to_all | solution.py:482
  37.4 0.0 copy-start.10
  37.4 0.0 copy-start.14
  37.4 0.0 copy-start.23
  37.5 6.6 %expert_forward.2 = bf16[64,2,8,384]{3,2,1,0:T(8,128)(2,1)S(1)} custom-call(bf16[64,2,8,384]{3,2,1,0:T(8,128)(2,1)S(1)} %bitcast.40, f32[1,768]{1,0:T(1,128)S(1)} %copy-done.18, bf16[768,1536]{1,0:T(8,128)(2,1)} %get-tuple-element.97.w_in, bf16[1536,768]{1,0:T(8,128)(2,1)S(1)} %copy-done.3), custom_call_target="tpu_custom_call" | custom-call | flops 2415919104 | bytes 6294528 | tf_op jit(solution)/shard_map/cond/branch_1_fun/expert_forward/pallas_call | solution.py:213
  44.1 0.0 copy-start.1
  44.1 24.6 %all_to_all.38 = bf16[128,8,384]{2,1,0:T(8,128)(2,1)S(1)} all-to-all(bf16[128,8,384]{2,1,0:T(8,128)(2,1)S(1)} %bitcast.38), channel_id=1, replica_groups=mesh['section'=2,'expert'=64,'head'=2] {'expert','head'}, dimensions={0} | all-to-all | bytes 1572864 | tf_op jit(solution)/shard_map/cond/branch_1_fun/all_to_all | solution.py:482
  68.7 0.4 gather.4
  69.1 0.1 collective-permute-start
  69.2 1.4 collective-permute-done
  70.6 12.2 %conditional.4 = (bf16[2,128,384]{2,1,0:T(8,128)(2,1)S(1)}, f32[512,1536]{1,0:T(8,128)}, bf16[64,2,8,384]{3,2,1,0:T(8,128)(2,1)}, bf16[512,1536]{1,0:T(8,128)(2,1)S(1)}) conditional(s32[]{:T(128)} %convert_element_type.2, (bf16[2,128,384]{2,1,0:T(8,128)(2,1)S(1)}, s32[2,128]{1,0:T(2,128)}, s32[2,128]{1,0:T(2,128)}, ...), branch_computations={%region_2.0_spmd, %region_3.0_spmd} | conditional | flops 3825205248 | bytes 31288524 | solution.py:524
  70.6 0.9 copy.18
  71.6 0.9 copy.20
  72.5 10.3 %slope.1 = f32[512,1536]{1,0:T(8,128)} custom-call(bf16[64,2,8,384]{3,2,1,0:T(8,128)(2,1)S(1)} %get-tuple-element.173.rows, f32[1,768]{1,0:T(1,128)} %get-tuple-element.112.gain, bf16[768,1536]{1,0:T(8,128)(2,1)} %get-tuple-element.113.w_in), custom_call_target="tpu_custom_call" | custom-call | flops 1207959552 | bytes 6294528 | tf_op jit(solution)/shard_map/cond/branch_1_fun/slope/pallas_call | solution.py:45
  82.7 0.1 broadcast.2
  82.8 45.6 %collective-permute-start.1 = (bf16[2,128,384]{2,1,0:T(8,128)(2,1)S(1)}, bf16[2,128,384]{2,1,0:T(8,128)(2,1)S(1)}, u32[]{:S(2)}, u32[]{:S(2)}) collective-permute-start(bf16[2,128,384]{2,1,0:T(8,128)(2,1)S(1)} %get-tuple-element.158), channel_id=1, source_target_pairs={{0,128},{128,0},{1,129},{129,1},{2,130},{130,2},{3,131},{131,3},{4... | collective-permute-start | bytes 589832 | tf_op jit(solution)/shard_map/ppermute | solution.py:487
  128.5 1.1 collective-permute-done.1
  129.5 57.9 %conditional.5 = (bf16[768,1536]{1,0:T(8,128)(2,1)}, bf16[1536,768]{1,0:T(8,128)(2,1)}, bf16[1,2,128,384]{3,2,1,0:T(8,128)(2,1)S(1)}) conditional(s32[]{:T(128)} %convert_element_type.2, (bf16[64,2,8,384]{3,2,1,0:T(8,128)(2,1)}, f32[1,768]{1,0:T(1,128)}, bf16[768,1536]{1,0:T(8,128)(2,1)}, bf16[1536,768]{1,0:T(8,128)(2,1)}, ...), branch_computations={%region_4.0_spmd, %region_5.0_spmd} | conditional | flops 6241124352 | bytes 40729796 | solution.py:540
  129.5 1.4 place.7
  131.0 24.4 %all_to_all.41 = bf16[128,8,384]{2,1,0:T(8,128)(2,1)S(1)} all-to-all(bf16[128,8,384]{2,1,0:T(8,128)(2,1)S(1)} %bitcast.30), channel_id=1, replica_groups=mesh['section'=2,'expert'=64,'head'=2] {'expert','head'}, dimensions={0} | all-to-all | bytes 1572864 | tf_op jit(solution)/shard_map/cond/branch_1_fun/all_to_all | solution.py:482
  155.4 6.3 %expert_backward.1 = (bf16[64,2,8,384]{3,2,1,0:T(8,128)(2,1)}, bf16[512,1536]{1,0:T(8,128)(2,1)S(1)}) custom-call(bf16[64,2,8,384]{3,2,1,0:T(8,128)(2,1)S(1)} %bitcast.34, f32[512,1536]{1,0:T(8,128)} %get-tuple-element.136.slope, bf16[768,1536]{1,0:T(8,128)(2,1)} %get-tuple-element.135.w_in, bf16[1536,768]{1,0:T(8,128)(2,1)S(1)} %copy-done.5, ...), custom_call_target="tpu_custom_call" | custom-call | flops 2415919104 | bytes 11799552 | tf_op jit(solution)/shard_map/cond/branch_1_fun/expert_backward/pallas_call | solution.py:213
  161.8 6.6 %all-to-all-start.6 = ((bf16[128,8,384]{2,1,0:T(8,128)(2,1)}), bf16[128,8,384]{2,1,0:T(8,128)(2,1)S(1)}, u32[]{:S(2)}, u32[]{:S(2)}) async-start(bf16[128,8,384]{2,1,0:T(8,128)(2,1)} %bitcast.17), calls=%async_computation.6 | async-start | bytes 1572864 | tf_op jit(solution)/shard_map/cond/branch_1_fun/all_to_all | solution.py:482
  168.4 0.0 copy-start.13
  168.4 9.2 %weight_grads.3 = (bf16[768,1536]{1,0:T(8,128)(2,1)}, bf16[1536,768]{1,0:T(8,128)(2,1)}) custom-call(bf16[64,2,8,384]{3,2,1,0:T(8,128)(2,1)} %copy-done.2, f32[1,768]{1,0:T(1,128)S(1)} %copy-done.21, bf16[64,2,8,384]{3,2,1,0:T(8,128)(2,1)S(1)} %bitcast.35, bf16[768,1536]{1,0:T(8,128)(2,1)} %get-tuple-element.135.w_in, ...), custom_call_target="tpu_custom_call" | custom-call | flops 3623878656 | bytes 10226688 | tf_op jit(solution)/shard_map/cond/branch_1_fun/weight_grads/pallas_call | solution.py:45
  177.5 9.1 %all-to-all-done.6 = bf16[128,8,384]{2,1,0:T(8,128)(2,1)S(1)} async-done(((bf16[128,8,384]{2,1,0:T(8,128)(2,1)}), bf16[128,8,384]{2,1,0:T(8,128)(2,1)S(1)}, u32[]{:S(2)}, u32[]{:S(2)}) %all-to-all-start.6) | async-done | bytes 786464 | tf_op jit(solution)/shard_map/cond/branch_1_fun/all_to_all | solution.py:482
  186.7 0.5 gather.7
  187.4 0.0 copy-start.9
  187.5 0.7 copy-done.9
  (21 shorter events, 0.0 us)
Async XLA Ops:
  0.7 36.8 %copy-start.3 = (bf16[1536,768]{1,0:T(8,128)(2,1)S(1)}, bf16[1536,768]{1,0:T(8,128)(2,1)}, u32[]{:S(2)}) copy-start(bf16[1536,768]{1,0:T(8,128)(2,1)} %get-tuple-element.98.w_out) | copy-start | bytes 7077892 | tf_op jit(solution)/shard_map/cond
  0.7 36.7 %copy-start.18 = (f32[1,768]{1,0:T(1,128)S(1)}, f32[1,768]{1,0:T(1,128)}, u32[]{:S(2)}) copy-start(f32[1,768]{1,0:T(1,128)} %get-tuple-element.96.gain) | copy-start | bytes 9220 | tf_op jit(solution)/shard_map/cond
  37.4 6.7 %copy-start = (bf16[128,8,384]{2,1,0:T(8,128)(2,1)}, bf16[128,8,384]{2,1,0:T(8,128)(2,1)S(1)}, u32[]{:S(2)}) copy-start(bf16[128,8,384]{2,1,0:T(8,128)(2,1)S(1)} %all_to_all.37) | copy-start | bytes 2359300 | tf_op jit(solution)/shard_map/cond
  37.4 31.3 %copy-start.7 = (bf16[2,128,384]{2,1,0:T(8,128)(2,1)S(1)}, bf16[2,128,384]{2,1,0:T(8,128)(2,1)}, u32[]{:S(2)}) copy-start(bf16[2,128,384]{2,1,0:T(8,128)(2,1)} %get-tuple-element.93.refs_0_.refs_4_) | copy-start | bytes 589828 | tf_op jit(solution)/shard_map/cond
  37.4 31.3 %copy-start.10 = (s32[2,128]{1,0:T(2,128)S(1)}, s32[2,128]{1,0:T(2,128)}, u32[]{:S(2)}) copy-start(s32[2,128]{1,0:T(2,128)} %get-tuple-element.94.refs_1_) | copy-start | bytes 3076 | tf_op jit(solution)/shard_map/cond
  37.4 31.3 %copy-start.14 = (s32[2,128]{1,0:T(2,128)S(1)}, s32[2,128]{1,0:T(2,128)}, u32[]{:S(2)}) copy-start(s32[2,128]{1,0:T(2,128)} %get-tuple-element.95.refs_2_) | copy-start | bytes 3076 | tf_op jit(solution)/shard_map/cond
  37.4 31.2 %copy-start.23 = (f32[2,128]{1,0:T(2,128)S(1)}, f32[2,128]{1,0:T(2,128)}, u32[]{:S(2)}) copy-start(f32[2,128]{1,0:T(2,128)} %get-tuple-element.99.refs_3_) | copy-start | bytes 3076 | tf_op jit(solution)/shard_map/cond
  44.1 25.0 %copy-start.1 = (bf16[128,8,384]{2,1,0:T(8,128)(2,1)S(1)}, bf16[128,8,384]{2,1,0:T(8,128)(2,1)}, u32[]{:S(2)}) copy-start(bf16[128,8,384]{2,1,0:T(8,128)(2,1)} %copy-done) | copy-start | bytes 2359300 | tf_op jit(solution)/shard_map/cond
  69.1 1.5 collective-permute-start
  70.6 58.9 %copy-start.22 = (f32[1,2,128]{2,1,0:T(2,128)S(1)}, f32[1,2,128]{2,1,0:T(2,128)}, u32[]{:S(2)}) copy-start(f32[1,2,128]{2,1,0:T(2,128)} %param.15) | copy-start | bytes 3076
  82.8 46.7 %collective-permute-start.1 = (bf16[2,128,384]{2,1,0:T(8,128)(2,1)S(1)}, bf16[2,128,384]{2,1,0:T(8,128)(2,1)S(1)}, u32[]{:S(2)}, u32[]{:S(2)}) collective-permute-start(bf16[2,128,384]{2,1,0:T(8,128)(2,1)S(1)} %get-tuple-element.158), channel_id=1, source_target_pairs={{0,128},{128,0},{1,129},{129,1},{2,130},{130,2},{3,131},{131,3},{4... | collective-permute-start | bytes 589832 | tf_op jit(solution)/shard_map/ppermute | solution.py:487
  129.5 32.2 %copy-start.2 = (bf16[64,2,8,384]{3,2,1,0:T(8,128)(2,1)}, bf16[64,2,8,384]{3,2,1,0:T(8,128)(2,1)S(1)}, u32[]{:S(2)}) copy-start(bf16[64,2,8,384]{3,2,1,0:T(8,128)(2,1)S(1)} %get-tuple-element.129.rows) | copy-start | bytes 2359300 | tf_op jit(solution)/shard_map/cond
  129.5 25.9 %copy-start.5 = (bf16[1536,768]{1,0:T(8,128)(2,1)S(1)}, bf16[1536,768]{1,0:T(8,128)(2,1)}, u32[]{:S(2)}) copy-start(bf16[1536,768]{1,0:T(8,128)(2,1)} %get-tuple-element.137.w_out) | copy-start | bytes 7077892 | tf_op jit(solution)/shard_map/cond
  129.5 25.9 %copy-start.21 = (f32[1,768]{1,0:T(1,128)S(1)}, f32[1,768]{1,0:T(1,128)}, u32[]{:S(2)}) copy-start(f32[1,768]{1,0:T(1,128)} %get-tuple-element.130.gain) | copy-start | bytes 9220 | tf_op jit(solution)/shard_map/cond
  161.8 24.9 %all-to-all-start.6 = ((bf16[128,8,384]{2,1,0:T(8,128)(2,1)}), bf16[128,8,384]{2,1,0:T(8,128)(2,1)S(1)}, u32[]{:S(2)}, u32[]{:S(2)}) async-start(bf16[128,8,384]{2,1,0:T(8,128)(2,1)} %bitcast.17), calls=%async_computation.6 | async-start | bytes 1572864 | tf_op jit(solution)/shard_map/cond/branch_1_fun/all_to_all | solution.py:482
  168.4 18.3 %copy-start.13 = (s32[2,128]{1,0:T(2,128)S(1)}, s32[2,128]{1,0:T(2,128)}, u32[]{:S(2)}) copy-start(s32[2,128]{1,0:T(2,128)} %get-tuple-element.132.refs_1_) | copy-start | bytes 3076 | tf_op jit(solution)/shard_map/cond
  168.4 18.3 %copy-start.17 = (s32[2,128]{1,0:T(2,128)S(1)}, s32[2,128]{1,0:T(2,128)}, u32[]{:S(2)}) copy-start(s32[2,128]{1,0:T(2,128)} %get-tuple-element.133.refs_2_) | copy-start | bytes 3076 | tf_op jit(solution)/shard_map/cond
  187.4 0.7 copy-start.9

commit v3 on v2

--- a/solution.py
+++ b/solution.py
@@ -167,7 +167,7 @@
     return pl.BlockSpec(shape, lambda j: (0,) * len(shape))
 
 
-CHUNK = 256
+CHUNK = 128
 NARROW = 128
 GROUPS = 2
 
@@ -224,12 +224,15 @@
     )(*ins)
 
 
-def forward_body(rows, gain, w_in, w_out, out, rows_v, w_in_v, w_out_v, normed, out_v, sems):
+def forward_body(rows, gain, w_in, w_out, out, kept, rows_v, w_in_v, w_out_v, normed, out_v, pre_v, sems):
     loads = copies_of([(rows, rows_v), (w_in, w_in_v), (w_out, w_out_v)], sems)
     start_all(loads)
 
     def stored(r):
         return pltpu.make_async_copy(expert_group(out_v, r), expert_group(out, r), sems.at[3 + r])
+
+    def saved(r):
+        return pltpu.make_async_copy(row_group(pre_v, r), row_group(kept, r), sems.at[3 + GROUPS + r])
 
     loads[0].wait()
 
@@ -241,7 +244,10 @@
         def _():
             loads[1].wait()
 
-        act = act_of(dot(normed[...], w_in_v[...])).astype(BF16)
+        pre = dot(normed[...], w_in_v[...])
+        row_group(pre_v, r)[...] = pre
+        saved(r).start()
+        act = act_of(pre).astype(BF16)
 
         @pl.when(r == 0)
         def _():
@@ -252,13 +258,14 @@
 
     for r in range(GROUPS):
         stored(r).wait()
+        saved(r).wait()
 
 
 def expert_forward(rows, gain, w_in, w_out):
     count, width, hidden = sizes(rows, w_in)
     return owned(
         forward_body,
-        [struct(rows.shape, BF16)],
+        [struct(rows.shape, BF16), struct((count, hidden), F32)],
         (rows, gain, w_in, w_out),
         4 * count * width * hidden,
         [
@@ -267,10 +274,11 @@
             (w_out.shape, BF16),
             ((count // GROUPS, width), BF16),
             (rows.shape, BF16),
+            ((count, hidden), F32),
         ],
-        3 + GROUPS,
+        3 + 2 * GROUPS,
         "expert_forward",
-    )[0]
+    )
 
 
 def grad_act_body(grads, w_out, out, flat):
@@ -297,38 +305,37 @@
     )[0]
 
 
-def slope_body(rows, gain, w_in, out, normed):
-    @pl.when(pl.program_id(0) == 0)
-    def _():
-        fill_normed(rows, gain, normed)
-
-    out[...] = act_and_slope(dot(normed[...], w_in[...]))[1]
-
-
-def slope_of_rows(rows, gain, w_in):
-    count, width, hidden = sizes(rows, w_in)
+def slope_body(pre, out):
+    out[...] = act_and_slope(pre[...])[1]
+
+
+def slope_of(pre):
+    count, hidden = pre.shape
+    block = pl.BlockSpec((NARROW, NARROW), lambda i, j: (i, j))
     return call(
         slope_body,
-        [struct((count, hidden), F32)],
-        (rows, gain, w_in),
-        2 * count * width * hidden,
-        grid=(hidden // NARROW,),
-        in_specs=[whole(rows.shape), whole(gain.shape), pl.BlockSpec((width, NARROW), lambda j: (0, j))],
-        out_specs=[pl.BlockSpec((count, NARROW), lambda j: (0, j))],
-        scratch=[pltpu.VMEM((count, width), BF16)],
+        [struct(pre.shape, F32)],
+        (pre,),
+        20 * count * hidden,
+        grid=(count // NARROW, hidden // NARROW),
+        in_specs=[block],
+        out_specs=[block],
         name="slope",
     )[0]
 
 
 def both_body(rows, gain, w_in, grad_act, out, kept, rows_v, w_in_v, ga_v, normed, pre_grad, out_v, sems):
-    loads = copies_of([(rows, rows_v), (w_in, w_in_v), (grad_act, ga_v)], sems)
+    loads = copies_of([(rows, rows_v), (w_in, w_in_v)], sems)
     start_all(loads)
 
+    def wide(r):
+        return pltpu.make_async_copy(row_group(grad_act, r), row_group(ga_v, r), sems.at[2 + r])
+
     def stored(r):
-        return pltpu.make_async_copy(expert_group(out_v, r), expert_group(out, r), sems.at[3 + r])
+        return pltpu.make_async_copy(expert_group(out_v, r), expert_group(out, r), sems.at[2 + GROUPS + r])
 
     def saved(r):
-        return pltpu.make_async_copy(row_group(pre_grad, r), row_group(kept, r), sems.at[3 + GROUPS + r])
+        return pltpu.make_async_copy(row_group(pre_grad, r), row_group(kept, r), sems.at[2 + 2 * GROUPS + r])
 
     loads[0].wait()
 
@@ -340,13 +347,12 @@
         @pl.when(r == 0)
         def _():
             loads[1].wait()
+            for g in range(GROUPS):
+                wide(g).start()
 
         slope = act_and_slope(dot(normed[...], w_in_v[...]))[1]
 
-        @pl.when(r == 0)
-        def _():
-            loads[2].wait()
-
+        wide(r).wait()
         pre = (row_group(ga_v, r)[...] * slope).astype(BF16)
         row_group(pre_grad, r)[...] = pre
         saved(r).start()
@@ -373,7 +379,7 @@
             ((count, hidden), BF16),
             (rows.shape, BF16),
         ],
-        3 + 2 * GROUPS,
+        2 + 3 * GROUPS,
         "expert_both",
     )
 
@@ -499,27 +505,27 @@
 
     def stage_one_lower():
         rows = exchange(place(local, ids, slots, None, experts, cap))
-        part = expert_forward(rows, norm_gain, w_in, w_out)
-        return gather(exchange(part), ids, slots, prob, local, cap), rows
+        part, pre = expert_forward(rows, norm_gain, w_in, w_out)
+        return gather(exchange(part), ids, slots, prob, local, cap), rows, pre
 
     def stage_one_upper():
         small, large = place(local, ids, slots, prob, experts, cap, (half // 3, half - half // 3))
         small, large = lax.optimization_barrier((exchange(small), large))
-        return local, jnp.concatenate([small, exchange(large)], axis=3)
-
-    sent, rows_one = lax.cond(first, stage_one_lower, stage_one_upper)
+        grads = jnp.concatenate([small, exchange(large)], axis=3)
+        return local, grads, grad_act_early(grads, w_out)
+
+    sent, rows_one, wide_one = lax.cond(first, stage_one_lower, stage_one_upper)
     hid = swap(sent)
 
     def stage_two_lower():
-        slope = slope_of_rows(rows_one, norm_gain, w_in)
+        slope = slope_of(wide_one)
         return local, slope, rows_one, jnp.zeros(slope.shape, BF16)
 
     def stage_two_upper():
         rows = exchange(place(hid, ids, slots, None, experts, cap))
-        grad_act = grad_act_early(rows_one, w_out)
-        back, pre_grad = expert_both(rows, norm_gain, w_in, grad_act)
+        back, pre_grad = expert_both(rows, norm_gain, w_in, wide_one)
         grad_hid = gather(exchange(back), ids, slots, None, local, cap)
-        return grad_hid, grad_act, rows, pre_grad
+        return grad_hid, wide_one, rows, pre_grad
 
     sent, wide, rows_two, pre_grad = lax.cond(first, stage_two_lower, stage_two_upper)
     grad_hid = swap(sent)
@@ -532,7 +538,7 @@
         return gather(got, ids, slots, None, grad_hid, cap), first_grad, second_grad
 
     def stage_three_upper():
-        part = expert_forward(rows_two, norm_gain, w_in, w_out)
+        part = expert_forward(rows_two, norm_gain, w_in, w_out)[0]
         first_grad, second_grad = weight_grads(rows_two, norm_gain, rows_one, w_in, pre_grad)
         part, first_grad, second_grad = lax.optimization_barrier((part, first_grad, second_grad))
         return gather(exchange(part), ids, slots, prob, hid, cap), first_grad, second_grad

time: 189 us -> 187 us (0.989)
  waiting for transfers between devices: 11.6 us -> 6.71 us
  starting transfers between devices: 52.3 us -> 55.2 us
    all_to_all x1, waiting for transfers between devices: 9.13 us -> 4.21 us  [exchange(): lax.all_to_all(flat, ('expert', 'head'), 0, 0, tiled=True)]
    ppermute x2, starting transfers between devices: 45.7 us -> 48.9 us  [swap(): lax.ppermute(block, 'section', [(i, (i + 1) % count) for i in range(count)])]
    pallas_call x2, Pallas kernels: 12.9 us -> 15.1 us  [owned(): pl.pallas_call(body, out_shape=outs, in_specs=[pl.BlockSpec(memory_space=...]
  transfers between devices with their start and end apart: 3 -> 3, of which waited for: 3 -> 3; matrix products, arithmetic and copies ran while one was open for 0% -> 0% of each run, Pallas kernels for 5% -> 8%
where the time goes in v3:
time: 187 us
  blocking collectives  84.4 us (45%)
  starting transfers between devices  55.2 us (30%)
  Pallas kernels  36.3 us (19%)
  waiting for transfers between devices  6.71 us (4%)
  local copies, waits for them, and re-layouts  3.1 us (2%)
    all_to_all x3, blocking collectives, exchange(): lax.all_to_all(flat, ('expert', 'head'), 0, 0, tiled=True)  84.4 us
    ppermute x2, starting transfers between devices, swap(): lax.ppermute(block, 'section', [(i, (i + 1) % count) for i in range(count)])  48.9 us
    pallas_call x6, Pallas kernels, call(): pl.pallas_call(body, out_shape=outs, scratch_shapes=scratch, compiler_par...  21.3 us
    pallas_call x2, Pallas kernels, owned(): pl.pallas_call(body, out_shape=outs, in_specs=[pl.BlockSpec(memory_space=...  15.1 us
    all_to_all x1, starting transfers between devices, exchange(): lax.all_to_all(flat, ('expert', 'head'), 0, 0, tiled=True)  6.34 us
    all_to_all x1, waiting for transfers between devices, exchange(): lax.all_to_all(flat, ('expert', 'head'), 0, 0, tiled=True)  4.21 us
  transfers between devices with their start and end apart: 3, of which 3 were waited for; matrix products, arithmetic and copies ran while one was open for 0% of the time, Pallas kernels for 8%

profile of v3, /device:TPU:32, one launch (start us, length us, event | category | flops | bytes accessed | tf_op | source)
XLA Modules:
  0.0 186.6 jit_solution(17219780914735530722)
XLA Ops:
  0.6 70.4 %conditional.3 = (bf16[2,128,384]{2,1,0:T(8,128)(2,1)S(1)}, bf16[64,2,8,384]{3,2,1,0:T(8,128)(2,1)}, f32[512,1536]{1,0:T(8,128)S(1)}) conditional(s32[]{:T(128)} %convert_element_type.2, (bf16[2,128,384]{2,1,0:T(8,128)(2,1)}, s32[2,128]{1,0:T(2,128)}, s32[2,128]{1,0:T(2,128)}, f32[2,128]{1,0:T(2,128)}, bf16[1536,768]{1,0:T(8,128)(2,1)}) %tuple.71, ...), branch_computations={%region_0.0_spmd, %region_1.0_spmd} | conditional | flops 2617245696 | bytes 25002176 | solution.py:517
  0.7 0.0 copy-start.1
  0.7 0.0 copy-start.21
  0.7 1.4 place.5
  2.1 35.4 %all_to_all.37 = bf16[128,8,384]{2,1,0:T(8,128)(2,1)} all-to-all(bf16[128,8,384]{2,1,0:T(8,128)(2,1)S(1)} %bitcast.33), channel_id=1, replica_groups=mesh['section'=2,'expert'=64,'head'=2] {'expert','head'}, dimensions={0} | all-to-all | bytes 1572864 | tf_op jit(solution)/shard_map/cond/branch_1_fun/all_to_all | solution.py:488
  37.5 0.0 copy-start.15
  37.5 0.0 copy-start.20
  37.5 8.6 %expert_forward.2 = (bf16[64,2,8,384]{3,2,1,0:T(8,128)(2,1)S(1)}, f32[512,1536]{1,0:T(8,128)S(1)}) custom-call(bf16[64,2,8,384]{3,2,1,0:T(8,128)(2,1)} %bitcast.5.rows, f32[1,768]{1,0:T(1,128)S(1)} %copy-done.21, bf16[768,1536]{1,0:T(8,128)(2,1)} %get-tuple-element.96.w_in, bf16[1536,768]{1,0:T(8,128)(2,1)S(1)} %copy-done.1), custom_call_target="tpu_custom_call" | custom-call | flops 2415919104 | bytes 9440256 | tf_op jit(solution)/shard_map/cond/branch_1_fun/expert_forward/pallas_call | solution.py:213
  46.2 24.4 %all_to_all.38 = bf16[128,8,384]{2,1,0:T(8,128)(2,1)S(1)} all-to-all(bf16[128,8,384]{2,1,0:T(8,128)(2,1)S(1)} %bitcast.38), channel_id=1, replica_groups=mesh['section'=2,'expert'=64,'head'=2] {'expert','head'}, dimensions={0} | all-to-all | bytes 1572864 | tf_op jit(solution)/shard_map/cond/branch_1_fun/all_to_all | solution.py:488
  70.6 0.4 gather.4
  71.0 0.3 collective-permute-start
  71.3 1.4 collective-permute-done
  72.7 5.7 %conditional.4 = (bf16[2,128,384]{2,1,0:T(8,128)(2,1)S(1)}, f32[512,1536]{1,0:T(8,128)S(1)}, bf16[64,2,8,384]{3,2,1,0:T(8,128)(2,1)S(1)}, bf16[512,1536]{1,0:T(8,128)(2,1)S(1)}) conditional(s32[]{:T(128)} %convert_element_type.2, (bf16[2,128,384]{2,1,0:T(8,128)(2,1)S(1)}, s32[2,128]{1,0:T(2,128)}, s32[2,128]{1,0:T(2,128)}, f32[1,768]{1,0:T(1,128)}, ...), branch_computations={%region_2.0_spmd, %region_3.0_spmd} | conditional | flops 2617245696 | bytes 24210604 | solution.py:530
  72.7 0.2 copy.31.pre
  72.9 0.7 copy-done.5
  73.7 1.1 copy.22
  74.8 3.5 %slope.1 = f32[512,1536]{1,0:T(8,128)S(1)} custom-call(f32[512,1536]{1,0:T(8,128)S(1)} %copy.31.pre), custom_call_target="tpu_custom_call" | custom-call | flops 15728640 | bytes 6291456 | tf_op jit(solution)/shard_map/cond/branch_1_fun/slope/pallas_call | solution.py:45
  78.4 0.1 broadcast.2
  78.5 48.6 %collective-permute-start.1 = (bf16[2,128,384]{2,1,0:T(8,128)(2,1)S(1)}, bf16[2,128,384]{2,1,0:T(8,128)(2,1)S(1)}, u32[]{:S(2)}, u32[]{:S(2)}) collective-permute-start(bf16[2,128,384]{2,1,0:T(8,128)(2,1)S(1)} %get-tuple-element.160), channel_id=1, source_target_pairs={{0,128},{128,0},{1,129},{129,1},{2,130},{130,2},{3,131},{131,3},{4... | collective-permute-start | bytes 589832 | tf_op jit(solution)/shard_map/ppermute | solution.py:493
  127.1 1.1 collective-permute-done.1
  128.2 57.7 %conditional.5 = (bf16[768,1536]{1,0:T(8,128)(2,1)}, bf16[1536,768]{1,0:T(8,128)(2,1)}, bf16[1,2,128,384]{3,2,1,0:T(8,128)(2,1)S(1)}) conditional(s32[]{:T(128)} %convert_element_type.2, (bf16[64,2,8,384]{3,2,1,0:T(8,128)(2,1)S(1)}, f32[1,768]{1,0:T(1,128)}, bf16[768,1536]{1,0:T(8,128)(2,1)}, bf16[1536,768]{1,0:T(8,128)(2,1)}, ...), branch_computations={%region_4.0_spmd, %region_5.0_spmd} | conditional | flops 6241124352 | bytes 50754808 | solution.py:546
  128.2 1.4 place.7
  129.6 0.2 copy-done
  129.8 24.6 %all_to_all.42 = bf16[128,8,384]{2,1,0:T(8,128)(2,1)S(1)} all-to-all(bf16[128,8,384]{2,1,0:T(8,128)(2,1)S(1)} %bitcast.30), channel_id=1, replica_groups=mesh['section'=2,'expert'=64,'head'=2] {'expert','head'}, dimensions={0} | all-to-all | bytes 1572864 | tf_op jit(solution)/shard_map/cond/branch_1_fun/all_to_all | solution.py:488
  154.4 6.4 %expert_backward.1 = (bf16[64,2,8,384]{3,2,1,0:T(8,128)(2,1)}, bf16[512,1536]{1,0:T(8,128)(2,1)S(1)}) custom-call(bf16[64,2,8,384]{3,2,1,0:T(8,128)(2,1)S(1)} %bitcast.35, f32[512,1536]{1,0:T(8,128)} %copy-done, bf16[768,1536]{1,0:T(8,128)(2,1)} %get-tuple-element.135.w_in, bf16[1536,768]{1,0:T(8,128)(2,1)S(1)} %copy-done.2, ...), custom_call_target="tpu_custom_call" | custom-call | flops 2415919104 | bytes 11799552 | tf_op jit(solution)/shard_map/cond/branch_1_fun/expert_backward/pallas_call | solution.py:213
  160.8 6.3 %all-to-all-start.6 = ((bf16[128,8,384]{2,1,0:T(8,128)(2,1)}), bf16[128,8,384]{2,1,0:T(8,128)(2,1)S(1)}, u32[]{:S(2)}, u32[]{:S(2)}) async-start(bf16[128,8,384]{2,1,0:T(8,128)(2,1)} %bitcast.17), calls=%async_computation.6 | async-start | bytes 1572864 | tf_op jit(solution)/shard_map/cond/branch_1_fun/all_to_all | solution.py:488
  167.2 0.0 copy-start.18
  167.2 14.0 %weight_grads.3 = (bf16[768,1536]{1,0:T(8,128)(2,1)}, bf16[1536,768]{1,0:T(8,128)(2,1)}) custom-call(bf16[64,2,8,384]{3,2,1,0:T(8,128)(2,1)} %get-tuple-element.129.rows, f32[1,768]{1,0:T(1,128)S(1)} %copy-done.24, bf16[64,2,8,384]{3,2,1,0:T(8,128)(2,1)S(1)} %bitcast.36, bf16[768,1536]{1,0:T(8,128)(2,1)} %get-tuple-element.135.w_in, ...), custom_call_target="tpu_custom_call" | custom-call | flops 3623878656 | bytes 10226688 | tf_op jit(solution)/shard_map/cond/branch_1_fun/weight_grads/pallas_call | solution.py:45
  181.2 4.2 %all-to-all-done.6 = bf16[128,8,384]{2,1,0:T(8,128)(2,1)S(1)} async-done(((bf16[128,8,384]{2,1,0:T(8,128)(2,1)}), bf16[128,8,384]{2,1,0:T(8,128)(2,1)S(1)}, u32[]{:S(2)}, u32[]{:S(2)}) %all-to-all-start.6) | async-done | bytes 786464 | tf_op jit(solution)/shard_map/cond/branch_1_fun/all_to_all | solution.py:488
  185.4 0.5 gather.7
  185.9 0.0 copy-start.10
  185.9 0.7 copy-done.10
  (20 shorter events, 0.1 us)
Async XLA Ops:
  0.7 36.9 %copy-start.1 = (bf16[1536,768]{1,0:T(8,128)(2,1)S(1)}, bf16[1536,768]{1,0:T(8,128)(2,1)}, u32[]{:S(2)}) copy-start(bf16[1536,768]{1,0:T(8,128)(2,1)} %get-tuple-element.97.w_out) | copy-start | bytes 7077892 | tf_op jit(solution)/shard_map/cond
  0.7 36.8 %copy-start.21 = (f32[1,768]{1,0:T(1,128)S(1)}, f32[1,768]{1,0:T(1,128)}, u32[]{:S(2)}) copy-start(f32[1,768]{1,0:T(1,128)} %get-tuple-element.95.gain) | copy-start | bytes 9220 | tf_op jit(solution)/shard_map/cond
  37.5 33.1 %copy-start.3 = (bf16[2,128,384]{2,1,0:T(8,128)(2,1)S(1)}, bf16[2,128,384]{2,1,0:T(8,128)(2,1)}, u32[]{:S(2)}) copy-start(bf16[2,128,384]{2,1,0:T(8,128)(2,1)} %get-tuple-element.92.refs_0_.refs_4_) | copy-start | bytes 589828 | tf_op jit(solution)/shard_map/cond
  37.5 33.1 %copy-start.11 = (s32[2,128]{1,0:T(2,128)S(1)}, s32[2,128]{1,0:T(2,128)}, u32[]{:S(2)}) copy-start(s32[2,128]{1,0:T(2,128)} %get-tuple-element.93.refs_1_) | copy-start | bytes 3076 | tf_op jit(solution)/shard_map/cond
  37.5 33.1 %copy-start.15 = (s32[2,128]{1,0:T(2,128)S(1)}, s32[2,128]{1,0:T(2,128)}, u32[]{:S(2)}) copy-start(s32[2,128]{1,0:T(2,128)} %get-tuple-element.94.refs_2_) | copy-start | bytes 3076 | tf_op jit(solution)/shard_map/cond
  37.5 33.1 %copy-start.20 = (f32[2,128]{1,0:T(2,128)S(1)}, f32[2,128]{1,0:T(2,128)}, u32[]{:S(2)}) copy-start(f32[2,128]{1,0:T(2,128)} %get-tuple-element.99.refs_3_) | copy-start | bytes 3076 | tf_op jit(solution)/shard_map/cond
  71.0 1.7 collective-permute-start
  72.7 55.4 %copy-start.19 = (f32[1,2,128]{2,1,0:T(2,128)S(1)}, f32[1,2,128]{2,1,0:T(2,128)}, u32[]{:S(2)}) copy-start(f32[1,2,128]{2,1,0:T(2,128)} %param.15) | copy-start | bytes 3076
  72.7 0.9 copy-start.5
  78.5 49.7 %collective-permute-start.1 = (bf16[2,128,384]{2,1,0:T(8,128)(2,1)S(1)}, bf16[2,128,384]{2,1,0:T(8,128)(2,1)S(1)}, u32[]{:S(2)}, u32[]{:S(2)}) collective-permute-start(bf16[2,128,384]{2,1,0:T(8,128)(2,1)S(1)} %get-tuple-element.160), channel_id=1, source_target_pairs={{0,128},{128,0},{1,129},{129,1},{2,130},{130,2},{3,131},{131,3},{4... | collective-permute-start | bytes 589832 | tf_op jit(solution)/shard_map/ppermute | solution.py:493
  128.2 1.6 copy-start
  128.2 26.2 %copy-start.2 = (bf16[1536,768]{1,0:T(8,128)(2,1)S(1)}, bf16[1536,768]{1,0:T(8,128)(2,1)}, u32[]{:S(2)}) copy-start(bf16[1536,768]{1,0:T(8,128)(2,1)} %get-tuple-element.137.w_out) | copy-start | bytes 7077892 | tf_op jit(solution)/shard_map/cond
  128.2 26.2 %copy-start.24 = (f32[1,768]{1,0:T(1,128)S(1)}, f32[1,768]{1,0:T(1,128)}, u32[]{:S(2)}) copy-start(f32[1,768]{1,0:T(1,128)} %get-tuple-element.130.gain) | copy-start | bytes 9220 | tf_op jit(solution)/shard_map/cond
  160.8 24.6 %all-to-all-start.6 = ((bf16[128,8,384]{2,1,0:T(8,128)(2,1)}), bf16[128,8,384]{2,1,0:T(8,128)(2,1)S(1)}, u32[]{:S(2)}, u32[]{:S(2)}) async-start(bf16[128,8,384]{2,1,0:T(8,128)(2,1)} %bitcast.17), calls=%async_computation.6 | async-start | bytes 1572864 | tf_op jit(solution)/shard_map/cond/branch_1_fun/all_to_all | solution.py:488
  167.2 18.3 %copy-start.14 = (s32[2,128]{1,0:T(2,128)S(1)}, s32[2,128]{1,0:T(2,128)}, u32[]{:S(2)}) copy-start(s32[2,128]{1,0:T(2,128)} %get-tuple-element.132.refs_1_) | copy-start | bytes 3076 | tf_op jit(solution)/shard_map/cond
  167.2 18.3 %copy-start.18 = (s32[2,128]{1,0:T(2,128)S(1)}, s32[2,128]{1,0:T(2,128)}, u32[]{:S(2)}) copy-start(s32[2,128]{1,0:T(2,128)} %get-tuple-element.133.refs_2_) | copy-start | bytes 3076 | tf_op jit(solution)/shard_map/cond
  185.9 0.7 copy-start.10
